TPU v7x, 32 devices: a whole 2x2x4 slice. The times are simulated.
32 devices in a mesh: row: 8 (over y, x, core), col: 4 (over z).
Axes of the slice: x: 2, y: 2, z: 4, core: 2. Of those that a mesh axis runs over, the one named last changes fastest.
Arguments:
- a_blocks: bfloat16 [8, 4, 64, 128, 128], P('row', 'col'), may hold values from -6 to 6
- b_blocks: bfloat16 [8, 4, 2, 24, 128, 128], P('row', 'col'), may hold values from -0.1796875 to 0.1796875
- a_index: int32 [8, 4, 8, 192], P('row', 'col'), may hold values from 0 to 63
- b_index: int32 [8, 4, 8, 192], P('row', 'col'), may hold values from 0 to 23
- c_index: int32 [8, 4, 8, 192], P('row', 'col'), may hold values from 0 to 63
- pair_count: int32 [8, 4, 8], P('row', 'col'), may hold values from 1 to 192, as said below
Outputs:
- c_blocks: bfloat16 [8, 4, 64, 128, 128], P('row', 'col')
Inputs may be any that keep to these rules, and one draw needn't show every extreme that they name: Only the first pair_count entries of each list are used; in every tick some C panel has all 192 entries live.
All inputs are finite; a program needn't handle non-finite values.
Results may differ from a plain program's by a relative error of at most 0.008.
Values may be sent and summed in bfloat16 or wider, within the bound.
No kernel may reach another device: no remote copies, remote signals or barrier semaphores. Data moves between devices by JAX's collectives and lax.ppermute only.
A program may use at most 192 MiB of HBM per device.

v0:
```python
import jax
import jax.numpy as jnp
from jax import lax
from jax.sharding import PartitionSpec as P

SLOTS_C = 64


def passed_along(value, axis, steps):
    count = lax.axis_size(axis)
    pairs = [(source, (source + steps) % count) for source in range(count)]
    return lax.ppermute(value, axis, pairs)


def select_blocks(panel, indices):
    slot_total = panel.shape[0]
    chooser = (indices[:, None] == jnp.arange(slot_total, dtype=jnp.int32)[None, :]).astype(
        jnp.bfloat16
    )
    flattened = panel.reshape(slot_total, -1)
    picked = jnp.dot(chooser, flattened, preferred_element_type=jnp.float32).astype(jnp.bfloat16)
    return picked.reshape(indices.shape[0], panel.shape[1], panel.shape[2])


def accumulate(running, products, c_list, live_mask):
    slot_total = running.shape[0]
    placer = (
        (c_list[None, :] == jnp.arange(slot_total, dtype=jnp.int32)[:, None]) & live_mask[None, :]
    ).astype(jnp.bfloat16)
    flattened = products.reshape(products.shape[0], -1)
    upper_part = flattened.astype(jnp.bfloat16)
    lower_part = (flattened - upper_part.astype(jnp.float32)).astype(jnp.bfloat16)
    added = jnp.dot(placer, upper_part, preferred_element_type=jnp.float32) + jnp.dot(
        placer, lower_part, preferred_element_type=jnp.float32
    )
    return running + added.reshape(running.shape)


def pair_products(a_panel, b_panel, a_list, b_list):
    a_rows = select_blocks(a_panel, a_list)
    b_rows = select_blocks(b_panel, b_list)
    return jnp.einsum("pik,pjk->pij", a_rows, b_rows, preferred_element_type=jnp.float32)


def padded_tick(running, a_panel, b_panel, a_list, b_list, c_list, live_count):
    products = pair_products(a_panel, b_panel, a_list, b_list)
    live_mask = jnp.arange(a_list.shape[0], dtype=jnp.int32) < live_count
    return accumulate(running, products, c_list, live_mask)


def per_device(a_blocks, b_blocks, a_index, b_index, c_index, pair_count):
    row_index = lax.axis_index("row")
    col_index = lax.axis_index("col")
    row_count = lax.axis_size("row")
    col_count = lax.axis_size("col")
    tick_total = a_index.shape[2]
    back_reach = tick_total // 2 - 1
    a_own = a_blocks[0, 0]
    b_own = b_blocks[0, 0]
    running = jnp.zeros((SLOTS_C, a_own.shape[1], a_own.shape[2]), jnp.float32)
    a_current = passed_along(a_own, "row", back_reach)
    b_current = passed_along(b_own, "col", back_reach)
    for tick in range(tick_total):
        if tick > 0:
            a_current = passed_along(a_current, "row", -1)
            b_current = passed_along(b_current, "col", -1)
        offset = tick - back_reach
        work_tick = offset + back_reach
        half_index = (row_index + col_index + offset) % row_count // col_count
        b_panel = lax.dynamic_index_in_dim(b_current, half_index, 0, keepdims=False)
        a_list = a_index[0, 0, work_tick]
        b_list = b_index[0, 0, work_tick]
        c_list = c_index[0, 0, work_tick]
        live_count = pair_count[0, 0, work_tick]
        running = padded_tick(running, a_current, b_panel, a_list, b_list, c_list, live_count)
    return running.astype(jnp.bfloat16)[None, None]


def solution(mesh):
    placed = (
        P("row", "col", None, None, None),
        P("row", "col", None, None, None, None),
        P("row", "col", None, None),
        P("row", "col", None, None),
        P("row", "col", None, None),
        P("row", "col", None),
    )
    return jax.shard_map(
        per_device,
        mesh=mesh,
        in_specs=placed,
        out_specs=P("row", "col", None, None, None),
        check_vma=False,
    )
```

profile of v0, /device:TPU:0, one launch (start us, length us, event | category | flops | bytes accessed | tf_op | source)
XLA Modules:
  0.0 488.5 jit_solution(14622909015959161596)
XLA Ops:
  19.2 21.6 %collective-permute-done.1 = bf16[2,24,128,128]{3,2,1,0:T(8,128)(2,1)} collective-permute-done((bf16[2,24,128,128]{3,2,1,0:T(8,128)(2,1)}, bf16[2,24,128,128]{3,2,1,0:T(8,128)(2,1)}, u32[]{:S(2)}, u32[]{:S(2)}) %collective-permute-start.1) | collective-permute-done | bytes 1572896 | tf_op jit(solution)/shard_map/ppermute | solution.py:12
  58.9 11.8 %fusion.159 = f32[192,128,128]{2,1,0:T(8,128)} fusion(bf16[192,128,128]{2,1,0:T(8,128)(2,1)} %bitcast.285, bf16[192,128,128]{2,1,0:T(8,128)(2,1)S(1)} %bitcast.283), kind=kOutput, calls=%fused_computation.213 | convolution fusion | flops 805306368 | bytes 25165824 | tf_op jit(solution)/shard_map/pik,pjk->pij/dot_general | solution.py:42
  70.8 11.7 %fusion.16 = f32[64,16384]{1,0:T(8,128)S(1)} fusion(f32[24,8,128,128]{3,2,1,0:T(8,128)} %bitcast.258, s32[192]{0:T(256)S(1)} %bitcast.314, pred[192]{0:T(512)(128)(4,1)S(1)} %iota_compare_fusion.47), kind=kOutput, calls=%fused_computation.56 | convolution fusion | flops 402677760 | bytes 16778176 | tf_op jit(solution)/shard_map/dot_general | solution.py:33
  82.5 12.3 %convolution_add_fusion.7 = f32[64,16384]{1,0:T(8,128)S(1)} fusion(f32[64,16384]{1,0:T(8,128)S(1)} %fusion.16, f32[24,8,128,128]{3,2,1,0:T(8,128)} %bitcast.259, s32[192]{0:T(256)S(1)} %bitcast.315, pred[192]{0:T(512)(128)(4,1)S(1)} %iota_compare_fusion.47), kind=kOutput, calls=%fused_computation.30 | convolution fusion | flops 416309248 | bytes 20972480 | tf_op jit(solution)/shard_map/dot_general | solution.py:33
  110.6 11.8 %fusion.160 = f32[192,128,128]{2,1,0:T(8,128)} fusion(bf16[192,128,128]{2,1,0:T(8,128)(2,1)} %bitcast.286, bf16[192,128,128]{2,1,0:T(8,128)(2,1)S(1)} %bitcast.282), kind=kOutput, calls=%fused_computation.214 | convolution fusion | flops 805306368 | bytes 25165824 | tf_op jit(solution)/shard_map/pik,pjk->pij/dot_general | solution.py:42
  122.4 11.7 %fusion.17 = f32[64,16384]{1,0:T(8,128)S(1)} fusion(f32[24,8,128,128]{3,2,1,0:T(8,128)} %bitcast.260, s32[192]{0:T(256)S(1)} %bitcast.312, pred[192]{0:T(512)(128)(4,1)S(1)} %iota_compare_fusion.46), kind=kOutput, calls=%fused_computation.57 | convolution fusion | flops 402677760 | bytes 16778176 | tf_op jit(solution)/shard_map/dot_general | solution.py:33
  141.5 14.2 %fusion.6 = f32[64,16384]{1,0:T(8,128)} fusion(f32[64,16384]{1,0:T(8,128)S(1)} %convolution_add_fusion.7, f32[64,16384]{1,0:T(8,128)S(1)} %fusion.17, f32[24,8,128,128]{3,2,1,0:T(8,128)} %bitcast.261, s32[192]{0:T(256)S(1)} %bitcast.313, pred[192]{0:T(512)(128)(4,1)S(1)} %iota_compare_fusion.46), kind=kOutput, calls=%fused_computation.29 | convolution fusion | flops 417357824 | bytes 25166784 | tf_op jit(solution)/shard_map/dot_general | solution.py:33
  169.0 11.8 %fusion.161 = f32[192,128,128]{2,1,0:T(8,128)} fusion(bf16[192,128,128]{2,1,0:T(8,128)(2,1)} %bitcast.287, bf16[192,128,128]{2,1,0:T(8,128)(2,1)S(1)} %bitcast.284), kind=kOutput, calls=%fused_computation.215 | convolution fusion | flops 805306368 | bytes 25165824 | tf_op jit(solution)/shard_map/pik,pjk->pij/dot_general | solution.py:42
  180.8 11.9 %fusion.18 = f32[64,16384]{1,0:T(8,128)S(1)} fusion(f32[24,8,128,128]{3,2,1,0:T(8,128)} %bitcast.262, s32[192]{0:T(256)S(1)} %bitcast.310, pred[192]{0:T(512)(128)(4,1)S(1)} %iota_compare_fusion.45), kind=kOutput, calls=%fused_computation.58 | convolution fusion | flops 402677760 | bytes 16778176 | tf_op jit(solution)/shard_map/dot_general | solution.py:33
  192.7 13.4 %fusion.5 = f32[64,16384]{1,0:T(8,128)S(1)} fusion(f32[64,16384]{1,0:T(8,128)S(1)} %copy-done, f32[64,16384]{1,0:T(8,128)S(1)} %fusion.18, f32[24,8,128,128]{3,2,1,0:T(8,128)} %bitcast.263, s32[192]{0:T(256)S(1)} %bitcast.311, pred[192]{0:T(512)(128)(4,1)S(1)} %iota_compare_fusion.45), kind=kOutput, calls=%fused_computation.27 | convolution fusion | flops 417357824 | bytes 25166784 | tf_op jit(solution)/shard_map/dot_general | solution.py:33
  235.9 11.8 %fusion.162 = f32[192,128,128]{2,1,0:T(8,128)} fusion(bf16[192,128,128]{2,1,0:T(8,128)(2,1)} %bitcast.288, bf16[192,128,128]{2,1,0:T(8,128)(2,1)S(1)} %bitcast.280), kind=kOutput, calls=%fused_computation.216 | convolution fusion | flops 805306368 | bytes 25165824 | tf_op jit(solution)/shard_map/pik,pjk->pij/dot_general | solution.py:42
  266.5 14.2 %fusion.4 = f32[64,16384]{1,0:T(8,128)} fusion(f32[64,16384]{1,0:T(8,128)S(1)} %fusion.5, f32[64,16384]{1,0:T(8,128)S(1)} %fusion.19, f32[24,8,128,128]{3,2,1,0:T(8,128)} %bitcast.265, s32[192]{0:T(256)S(1)} %bitcast.309, pred[192]{0:T(512)(128)(4,1)S(1)} %iota_compare_fusion.44), kind=kOutput, calls=%fused_computation.25 | convolution fusion | flops 417357824 | bytes 25166784 | tf_op jit(solution)/shard_map/dot_general | solution.py:33
  293.8 13.6 %fusion.163 = f32[192,128,128]{2,1,0:T(8,128)} fusion(bf16[192,128,128]{2,1,0:T(8,128)(2,1)} %bitcast.289, bf16[192,128,128]{2,1,0:T(8,128)(2,1)} %bitcast.273), kind=kOutput, calls=%fused_computation.217 | convolution fusion | flops 805306368 | bytes 25165824 | tf_op jit(solution)/shard_map/pik,pjk->pij/dot_general | solution.py:42
  307.5 11.9 %fusion.20 = f32[64,16384]{1,0:T(8,128)S(1)} fusion(f32[24,8,128,128]{3,2,1,0:T(8,128)} %bitcast.266, s32[192]{0:T(256)S(1)} %bitcast.306, pred[192]{0:T(512)(128)(4,1)S(1)} %iota_compare_fusion.43), kind=kOutput, calls=%fused_computation.60 | convolution fusion | flops 402677760 | bytes 16778176 | tf_op jit(solution)/shard_map/dot_general | solution.py:33
  319.3 13.7 %fusion.3 = f32[64,16384]{1,0:T(8,128)S(1)} fusion(f32[64,16384]{1,0:T(8,128)S(1)} %copy-done.1, f32[64,16384]{1,0:T(8,128)S(1)} %fusion.20, f32[24,8,128,128]{3,2,1,0:T(8,128)} %bitcast.267, s32[192]{0:T(256)S(1)} %bitcast.307, pred[192]{0:T(512)(128)(4,1)S(1)} %iota_compare_fusion.43), kind=kOutput, calls=%fused_computation.23 | convolution fusion | flops 417357824 | bytes 25166784 | tf_op jit(solution)/shard_map/dot_general | solution.py:33
  356.5 11.8 %fusion.164 = f32[192,128,128]{2,1,0:T(8,128)} fusion(bf16[192,128,128]{2,1,0:T(8,128)(2,1)} %bitcast.281, bf16[192,128,128]{2,1,0:T(8,128)(2,1)S(1)} %bitcast.272), kind=kOutput, calls=%fused_computation.218 | convolution fusion | flops 805306368 | bytes 25165824 | tf_op jit(solution)/shard_map/pik,pjk->pij/dot_general | solution.py:42
  368.3 11.7 %fusion.21 = f32[64,16384]{1,0:T(8,128)S(1)} fusion(f32[24,8,128,128]{3,2,1,0:T(8,128)} %bitcast.268, s32[192]{0:T(256)S(1)} %bitcast.304, pred[192]{0:T(512)(128)(4,1)S(1)} %copy-done.12), kind=kOutput, calls=%fused_computation.61 | convolution fusion | flops 402677760 | bytes 16778176 | tf_op jit(solution)/shard_map/dot_general | solution.py:33
  380.0 14.3 %fusion.2 = f32[64,16384]{1,0:T(8,128)} fusion(f32[64,16384]{1,0:T(8,128)S(1)} %fusion.3, f32[64,16384]{1,0:T(8,128)S(1)} %fusion.21, f32[24,8,128,128]{3,2,1,0:T(8,128)} %bitcast.269, s32[192]{0:T(256)S(1)} %bitcast.305, pred[192]{0:T(512)(128)(4,1)S(1)} %copy-done.12), kind=kOutput, calls=%fused_computation.21 | convolution fusion | flops 417357824 | bytes 25166784 | tf_op jit(solution)/shard_map/dot_general | solution.py:33
  404.8 11.8 %fusion.165 = f32[192,128,128]{2,1,0:T(8,128)} fusion(bf16[192,128,128]{2,1,0:T(8,128)(2,1)} %bitcast.290, bf16[192,128,128]{2,1,0:T(8,128)(2,1)S(1)} %bitcast.276), kind=kOutput, calls=%fused_computation.219 | convolution fusion | flops 805306368 | bytes 25165824 | tf_op jit(solution)/shard_map/pik,pjk->pij/dot_general | solution.py:42
  416.7 11.9 %fusion.22 = f32[64,16384]{1,0:T(8,128)S(1)} fusion(f32[24,8,128,128]{3,2,1,0:T(8,128)} %bitcast.270, s32[192]{0:T(256)S(1)} %bitcast.302, pred[192]{0:T(512)(128)(4,1)S(1)} %copy-done.11), kind=kOutput, calls=%fused_computation.62 | convolution fusion | flops 402677760 | bytes 16778176 | tf_op jit(solution)/shard_map/dot_general | solution.py:33
  428.5 13.4 %fusion.1 = f32[64,16384]{1,0:T(8,128)S(1)} fusion(f32[64,16384]{1,0:T(8,128)S(1)} %copy-done.2, f32[64,16384]{1,0:T(8,128)S(1)} %fusion.22, f32[24,8,128,128]{3,2,1,0:T(8,128)} %bitcast.271, s32[192]{0:T(256)S(1)} %bitcast.303, pred[192]{0:T(512)(128)(4,1)S(1)} %copy-done.11), kind=kOutput, calls=%fused_computation.19 | convolution fusion | flops 417357824 | bytes 25166784 | tf_op jit(solution)/shard_map/dot_general | solution.py:33
  450.2 11.8 %fusion.166 = f32[192,128,128]{2,1,0:T(8,128)} fusion(bf16[192,128,128]{2,1,0:T(8,128)(2,1)} %bitcast.291, bf16[192,128,128]{2,1,0:T(8,128)(2,1)S(1)} %bitcast.279), kind=kOutput, calls=%fused_computation.220 | convolution fusion | flops 805306368 | bytes 25165824 | tf_op jit(solution)/shard_map/pik,pjk->pij/dot_general | solution.py:42
  462.1 11.9 %fusion.23 = f32[64,16384]{1,0:T(8,128)S(1)} fusion(f32[24,8,128,128]{3,2,1,0:T(8,128)} %bitcast.256, s32[192]{0:T(256)S(1)} %bitcast.300, pred[192]{0:T(512)(128)(4,1)S(1)} %copy-done.10), kind=kOutput, calls=%fused_computation.63 | convolution fusion | flops 402677760 | bytes 16778176 | tf_op jit(solution)/shard_map/dot_general | solution.py:33
  474.0 12.4 %fusion.64 = bf16[8,8,128,128]{3,1,2,0:T(8,128)(2,1)S(1)} fusion(f32[64,16384]{1,0:T(8,128)S(1)} %fusion.1, f32[64,16384]{1,0:T(8,128)S(1)} %fusion.23, f32[24,8,128,128]{3,2,1,0:T(8,128)} %bitcast.257, s32[192]{0:T(256)S(1)} %bitcast.301, pred[192]{0:T(512)(128)(4,1)S(1)} %copy-done.10), kind=kOutput, calls=%fused_computation.96 | convolution fusion | flops 418406400 | bytes 23069632 | tf_op jit(solution)/shard_map/dot_general | solution.py:33
  (121 shorter events, 179.3 us)
Async XLA Ops:
  0.0 50.1 %collective-permute-start = (bf16[64,128,128]{2,1,0:T(8,128)(2,1)}, bf16[64,128,128]{2,1,0:T(8,128)(2,1)}, u32[]{:S(2)}, u32[]{:S(2)}) collective-permute-start(bf16[64,128,128]{2,1,0:T(8,128)(2,1)} %bitcast.332), channel_id=1, source_target_pairs={{0,12},{4,16},{8,20},{12,24},{16,28},{20,0},{24,4},{28,8},{1,13},{... | collective-permute-start | bytes 6291464 | tf_op jit(solution)/shard_map/ppermute | solution.py:12
  2.4 38.4 %collective-permute-start.1 = (bf16[2,24,128,128]{3,2,1,0:T(8,128)(2,1)}, bf16[2,24,128,128]{3,2,1,0:T(8,128)(2,1)}, u32[]{:S(2)}, u32[]{:S(2)}) collective-permute-start(bf16[2,24,128,128]{3,2,1,0:T(8,128)(2,1)} %bitcast.333), channel_id=1, source_target_pairs={{0,3},{1,0},{2,1},{3,2},{4,7},{5,4},{6,5},{7,6},{8,11},{9,8},{10,9... | collective-permute-start | bytes 4718600 | tf_op jit(solution)/shard_map/ppermute | solution.py:12
  45.8 49.0 %collective-permute-start.3 = (bf16[2,24,128,128]{3,2,1,0:T(8,128)(2,1)}, bf16[2,24,128,128]{3,2,1,0:T(8,128)(2,1)}, u32[]{:S(2)}, u32[]{:S(2)}) collective-permute-start(bf16[2,24,128,128]{3,2,1,0:T(8,128)(2,1)} %collective-permute-done.1), channel_id=1, source_target_pairs={{0,3},{1,0},{2,1},{3,2},{4,7},{5,4},{6,5},{7,6},{8,11},{9,8},{10,9... | collective-permute-start | bytes 4718600 | tf_op jit(solution)/shard_map/ppermute | solution.py:12
  58.1 44.3 %collective-permute-start.2 = (bf16[64,128,128]{2,1,0:T(8,128)(2,1)}, bf16[64,128,128]{2,1,0:T(8,128)(2,1)}, u32[]{:S(2)}, u32[]{:S(2)}) collective-permute-start(bf16[64,128,128]{2,1,0:T(8,128)(2,1)} %collective-permute-done), channel_id=1, source_target_pairs={{0,28},{4,0},{8,4},{12,8},{16,12},{20,16},{24,20},{28,24},{1,29},{... | collective-permute-start | bytes 6291464 | tf_op jit(solution)/shard_map/ppermute | solution.py:12
  99.7 37.3 %collective-permute-start.5 = (bf16[2,24,128,128]{3,2,1,0:T(8,128)(2,1)}, bf16[2,24,128,128]{3,2,1,0:T(8,128)(2,1)}, u32[]{:S(2)}, u32[]{:S(2)}) collective-permute-start(bf16[2,24,128,128]{3,2,1,0:T(8,128)(2,1)} %collective-permute-done.3), channel_id=1, source_target_pairs={{0,3},{1,0},{2,1},{3,2},{4,7},{5,4},{6,5},{7,6},{8,11},{9,8},{10,9... | collective-permute-start | bytes 4718600 | tf_op jit(solution)/shard_map/ppermute | solution.py:12
  110.4 50.2 %collective-permute-start.4 = (bf16[64,128,128]{2,1,0:T(8,128)(2,1)}, bf16[64,128,128]{2,1,0:T(8,128)(2,1)}, u32[]{:S(2)}, u32[]{:S(2)}) collective-permute-start(bf16[64,128,128]{2,1,0:T(8,128)(2,1)} %collective-permute-done.2), channel_id=1, source_target_pairs={{0,28},{4,0},{8,4},{12,8},{16,12},{20,16},{24,20},{28,24},{1,29},{... | collective-permute-start | bytes 6291464 | tf_op jit(solution)/shard_map/ppermute | solution.py:12
  137.0 43.8 %collective-permute-start.7 = (bf16[2,24,128,128]{3,2,1,0:T(8,128)(2,1)}, bf16[2,24,128,128]{3,2,1,0:T(8,128)(2,1)}, u32[]{:S(2)}, u32[]{:S(2)}) collective-permute-start(bf16[2,24,128,128]{3,2,1,0:T(8,128)(2,1)} %collective-permute-done.5), channel_id=1, source_target_pairs={{0,3},{1,0},{2,1},{3,2},{4,7},{5,4},{6,5},{7,6},{8,11},{9,8},{10,9... | collective-permute-start | bytes 4718600 | tf_op jit(solution)/shard_map/ppermute | solution.py:12
  169.0 58.8 %collective-permute-start.6 = (bf16[64,128,128]{2,1,0:T(8,128)(2,1)}, bf16[64,128,128]{2,1,0:T(8,128)(2,1)}, u32[]{:S(2)}, u32[]{:S(2)}) collective-permute-start(bf16[64,128,128]{2,1,0:T(8,128)(2,1)} %collective-permute-done.4), channel_id=1, source_target_pairs={{0,28},{4,0},{8,4},{12,8},{16,12},{20,16},{24,20},{28,24},{1,29},{... | collective-permute-start | bytes 6291464 | tf_op jit(solution)/shard_map/ppermute | solution.py:12
  180.8 11.9 %copy-start = (f32[64,16384]{1,0:T(8,128)S(1)}, f32[64,16384]{1,0:T(8,128)}, u32[]{:S(2)}) copy-start(f32[64,16384]{1,0:T(8,128)} %fusion.6) | copy-start | bytes 12582916
  180.8 37.1 %collective-permute-start.9 = (bf16[2,24,128,128]{3,2,1,0:T(8,128)(2,1)}, bf16[2,24,128,128]{3,2,1,0:T(8,128)(2,1)}, u32[]{:S(2)}, u32[]{:S(2)}) collective-permute-start(bf16[2,24,128,128]{3,2,1,0:T(8,128)(2,1)} %collective-permute-done.7), channel_id=1, source_target_pairs={{0,3},{1,0},{2,1},{3,2},{4,7},{5,4},{6,5},{7,6},{8,11},{9,8},{10,9... | collective-permute-start | bytes 4718600 | tf_op jit(solution)/shard_map/ppermute | solution.py:12
  225.5 36.5 %collective-permute-start.11 = (bf16[2,24,128,128]{3,2,1,0:T(8,128)(2,1)}, bf16[2,24,128,128]{3,2,1,0:T(8,128)(2,1)}, u32[]{:S(2)}, u32[]{:S(2)}) collective-permute-start(bf16[2,24,128,128]{3,2,1,0:T(8,128)(2,1)} %collective-permute-done.9), channel_id=1, source_target_pairs={{0,3},{1,0},{2,1},{3,2},{4,7},{5,4},{6,5},{7,6},{8,11},{9,8},{10,9... | collective-permute-start | bytes 4718600 | tf_op jit(solution)/shard_map/ppermute | solution.py:12
  235.8 49.7 %collective-permute-start.8 = (bf16[64,128,128]{2,1,0:T(8,128)(2,1)}, bf16[64,128,128]{2,1,0:T(8,128)(2,1)}, u32[]{:S(2)}, u32[]{:S(2)}) collective-permute-start(bf16[64,128,128]{2,1,0:T(8,128)(2,1)} %collective-permute-done.6), channel_id=1, source_target_pairs={{0,28},{4,0},{8,4},{12,8},{16,12},{20,16},{24,20},{28,24},{1,29},{... | collective-permute-start | bytes 6291464 | tf_op jit(solution)/shard_map/ppermute | solution.py:12
  262.0 45.4 %collective-permute-start.13 = (bf16[2,24,128,128]{3,2,1,0:T(8,128)(2,1)}, bf16[2,24,128,128]{3,2,1,0:T(8,128)(2,1)}, u32[]{:S(2)}, u32[]{:S(2)}) collective-permute-start(bf16[2,24,128,128]{3,2,1,0:T(8,128)(2,1)} %collective-permute-done.11), channel_id=1, source_target_pairs={{0,3},{1,0},{2,1},{3,2},{4,7},{5,4},{6,5},{7,6},{8,11},{9,8},{10,9... | collective-permute-start | bytes 4718600 | tf_op jit(solution)/shard_map/ppermute | solution.py:12
  293.8 46.8 %collective-permute-start.10 = (bf16[64,128,128]{2,1,0:T(8,128)(2,1)}, bf16[64,128,128]{2,1,0:T(8,128)(2,1)}, u32[]{:S(2)}, u32[]{:S(2)}) collective-permute-start(bf16[64,128,128]{2,1,0:T(8,128)(2,1)} %collective-permute-done.8), channel_id=1, source_target_pairs={{0,28},{4,0},{8,4},{12,8},{16,12},{20,16},{24,20},{28,24},{1,29},{... | collective-permute-start | bytes 6291464 | tf_op jit(solution)/shard_map/ppermute | solution.py:12
  307.4 11.9 %copy-start.1 = (f32[64,16384]{1,0:T(8,128)S(1)}, f32[64,16384]{1,0:T(8,128)}, u32[]{:S(2)}) copy-start(f32[64,16384]{1,0:T(8,128)} %fusion.4) | copy-start | bytes 12582916
  307.4 41.3 %collective-permute-start.15 = (bf16[2,24,128,128]{3,2,1,0:T(8,128)(2,1)}, bf16[2,24,128,128]{3,2,1,0:T(8,128)(2,1)}, u32[]{:S(2)}, u32[]{:S(2)}) collective-permute-start(bf16[2,24,128,128]{3,2,1,0:T(8,128)(2,1)} %collective-permute-done.13), channel_id=1, source_target_pairs={{0,3},{1,0},{2,1},{3,2},{4,7},{5,4},{6,5},{7,6},{8,11},{9,8},{10,9... | collective-permute-start | bytes 4718600 | tf_op jit(solution)/shard_map/ppermute | solution.py:12
  356.3 38.1 %collective-permute-start.12 = (bf16[64,128,128]{2,1,0:T(8,128)(2,1)}, bf16[64,128,128]{2,1,0:T(8,128)(2,1)}, u32[]{:S(2)}, u32[]{:S(2)}) collective-permute-start(bf16[64,128,128]{2,1,0:T(8,128)(2,1)} %collective-permute-done.10), channel_id=1, source_target_pairs={{0,28},{4,0},{8,4},{12,8},{16,12},{20,16},{24,20},{28,24},{1,29},{... | collective-permute-start | bytes 6291464 | tf_op jit(solution)/shard_map/ppermute | solution.py:12
  356.5 11.9 %copy-start.5 = (s32[1,1,1,192]{3,2,1,0:T(1,128)S(1)}, s32[1,1,1,192]{3,2,1,0:T(1,128)}, u32[]{:S(2)}) copy-start(s32[1,1,1,192]{3,2,1,0:T(1,128)} %get-tuple-element.6) | copy-start | bytes 2308
  380.0 14.3 %copy-start.7 = (s32[1,1,1,192]{3,2,1,0:T(1,128)S(1)}, s32[1,1,1,192]{3,2,1,0:T(1,128)}, u32[]{:S(2)}) copy-start(s32[1,1,1,192]{3,2,1,0:T(1,128)} %get-tuple-element.28) | copy-start | bytes 2308
  402.7 39.3 %collective-permute-start.14 = (bf16[64,128,128]{2,1,0:T(8,128)(2,1)}, bf16[64,128,128]{2,1,0:T(8,128)(2,1)}, u32[]{:S(2)}, u32[]{:S(2)}) collective-permute-start(bf16[64,128,128]{2,1,0:T(8,128)(2,1)} %collective-permute-done.12), channel_id=1, source_target_pairs={{0,28},{4,0},{8,4},{12,8},{16,12},{20,16},{24,20},{28,24},{1,29},{... | collective-permute-start | bytes 6291464 | tf_op jit(solution)/shard_map/ppermute | solution.py:12
  416.6 11.9 %copy-start.2 = (f32[64,16384]{1,0:T(8,128)S(1)}, f32[64,16384]{1,0:T(8,128)}, u32[]{:S(2)}) copy-start(f32[64,16384]{1,0:T(8,128)} %fusion.2) | copy-start | bytes 12582916
  428.5 13.5 %copy-start.6 = (s32[1,1,1,192]{3,2,1,0:T(1,128)S(1)}, s32[1,1,1,192]{3,2,1,0:T(1,128)}, u32[]{:S(2)}) copy-start(s32[1,1,1,192]{3,2,1,0:T(1,128)} %get-tuple-element.21) | copy-start | bytes 2308
  450.2 11.9 %copy-start.3 = (s32[1,1,1,192]{3,2,1,0:T(1,128)S(1)}, s32[1,1,1,192]{3,2,1,0:T(1,128)}, u32[]{:S(2)}) copy-start(s32[1,1,1,192]{3,2,1,0:T(1,128)} %get-tuple-element.5) | copy-start | bytes 2308
  450.2 11.9 %copy-start.10 = (pred[192]{0:T(512)(128)(4,1)S(1)}, pred[192]{0:T(512)(128)(4,1)}, u32[]{:S(2)}) copy-start(pred[192]{0:T(512)(128)(4,1)} %iota_compare_fusion.40) | copy-start | bytes 580
  (9 other events, 75.9 us)
where the time goes:
time: 495 us; the launch traced here: 489 us
  matrix products  342 us (69%)
  local copies, waits for them, and re-layouts  78.1 us (16%)
  waiting for transfers between devices  34 us (7%)
  starting transfers between devices  27.4 us (6%)
  other arithmetic  6.66 us (1%)
    dot_general x8, matrix products, accumulate(): jnp.dot(placer, lower_part, preferred_element_type=jnp.float32)  108 us
    dot_general x8, matrix products, pair_products(): jnp.einsum('pik,pjk->pij', a_rows, b_rows, preferred_element_type=jnp.flo...  96.4 us
    dot_general x8, matrix products, accumulate(): jnp.dot(placer, upper_part, preferred_element_type=jnp.float32)  94.4 us
    unnamed x51, local copies, waits for them, and re-layouts  62.1 us
    dot_general x16, matrix products, select_blocks(): jnp.dot(chooser, flattened, preferred_element_type=jnp.float32)  43 us
    ppermute x16, waiting for transfers between devices, passed_along(): return lax.ppermute(value, axis, pairs)  34 us
    ppermute x16, starting transfers between devices, passed_along(): return lax.ppermute(value, axis, pairs)  27.4 us
  transfers between devices with their start and end apart: 16, of which 4 were waited for; matrix products, arithmetic and copies ran while one was open for 75% of the time, Pallas kernels for 0%

commit v1 on v0

v1 whole, which is shorter than its diff:
```python
import functools

import jax
import jax.numpy as jnp
import numpy as np
from jax import lax
from jax.experimental import pallas as pl
from jax.experimental.pallas import tpu as pltpu
from jax.sharding import PartitionSpec as P

SLOTS_C = 64
GROUP = 16
FIELDS = 32
B_SHIFT, C_SHIFT = 8, 16
HBM = pl.BlockSpec(memory_space=pltpu.HBM)


def stage_kernel(table, counts, packed, *refs, stage, a_views, b_views, n_inputs, first, last):
    inputs = refs[:n_inputs]
    rest = refs[n_inputs:]
    c_in, rest = (None, rest) if first else (rest[0], rest[1:])
    out, total, a_buf, b_buf, b_turned, a_sem, b_sem, c_sem = rest[:8]
    rounded = rest[8] if last else None
    base = stage * FIELDS
    entries = table[base]
    slots_c = SLOTS_C

    def fetch(k, slot):
        a_id = table[base + 2 + 3 * k]
        b_id = table[base + 3 + 3 * k]
        for number, pieces in enumerate(a_views):

            @pl.when(a_id == number)
            def _(pieces=pieces):
                for ref_number, offset, size in pieces:
                    pltpu.make_async_copy(
                        inputs[ref_number], a_buf.at[slot, pl.ds(offset, size)], a_sem.at[slot]
                    ).start()

        for number, (ref_number, half) in enumerate(b_views):

            @pl.when(b_id == number)
            def _(ref_number=ref_number, half=half):
                source = inputs[ref_number] if half is None else inputs[ref_number].at[half]
                pltpu.make_async_copy(source, b_buf.at[slot], b_sem.at[slot]).start()

    def await_fetch(slot):
        pltpu.make_async_copy(a_buf.at[slot], a_buf.at[slot], a_sem.at[slot]).wait()
        pltpu.make_async_copy(b_buf.at[slot], b_buf.at[slot], b_sem.at[slot]).wait()

    if not first:
        brought = pltpu.make_async_copy(c_in, total.at[pl.ds(0, slots_c)], c_sem.at[0])
        brought.start()

    @pl.when(entries > 0)
    def _():
        fetch(0, 0)

    if first:
        total[...] = jnp.zeros_like(total)
    else:
        total[pl.ds(slots_c, 1)] = jnp.zeros_like(total[pl.ds(slots_c, 1)])
        brought.wait()

    def one_tick(k, carry):
        slot = lax.rem(k, 2)
        await_fetch(slot)

        @pl.when(k + 1 < entries)
        def _():
            fetch(k + 1, 1 - slot)

        tick = table[base + 1 + 3 * k]
        for s in range(b_buf.shape[1]):
            b_turned[s] = b_buf[slot, s].T

        def one_group(g, carry):
            for u in range(GROUP):
                word = packed[tick, g * GROUP + u]
                a_at = word & 255
                b_at = (word >> B_SHIFT) & 255
                c_at = word >> C_SHIFT
                product = jnp.dot(a_buf[slot, a_at], b_turned[b_at], preferred_element_type=jnp.float32)
                total[c_at] = total[c_at] + product
            return carry

        lax.fori_loop(0, (counts[tick] + GROUP - 1) // GROUP, one_group, 0)
        return carry

    lax.fori_loop(0, entries, one_tick, 0)

    if last:
        chunk = 16
        copies = []
        for start in range(0, slots_c, chunk):
            part = pl.ds(start, chunk)
            rounded[part] = total[part].astype(jnp.bfloat16)
            copies.append(pltpu.make_async_copy(rounded.at[part], out.at[part], c_sem.at[start // chunk]))
            copies[-1].start()
        for copy in copies:
            copy.wait()
    else:
        done = pltpu.make_async_copy(total.at[pl.ds(0, slots_c)], out, c_sem.at[0])
        done.start()
        done.wait()


def run_stage(stage, table, counts, packed, arrays, a_views, b_views, c_in, last, pairs_hint):
    first = c_in is None
    slots_a = max(sum(piece[2] for piece in pieces) for pieces in a_views)
    slots_b, bs = arrays[b_views[0][0]].shape[-3:-1]
    operands = list(arrays) + ([] if first else [c_in])
    kernel = functools.partial(
        stage_kernel,
        stage=stage,
        a_views=a_views,
        b_views=b_views,
        n_inputs=len(arrays),
        first=first,
        last=last,
    )
    scratch = [
        pltpu.VMEM((SLOTS_C + 1, bs, bs), jnp.float32),
        pltpu.VMEM((2, slots_a, bs, bs), jnp.bfloat16),
        pltpu.VMEM((2, slots_b, bs, bs), jnp.bfloat16),
        pltpu.VMEM((slots_b, bs, bs), jnp.bfloat16),
        pltpu.SemaphoreType.DMA((2,)),
        pltpu.SemaphoreType.DMA((2,)),
        pltpu.SemaphoreType.DMA((4,)),
    ]
    if last:
        scratch.append(pltpu.VMEM((SLOTS_C, bs, bs), jnp.bfloat16))
    return pl.pallas_call(
        kernel,
        out_shape=jax.ShapeDtypeStruct((SLOTS_C, bs, bs), jnp.bfloat16 if last else jnp.float32),
        grid_spec=pltpu.PrefetchScalarGridSpec(
            num_scalar_prefetch=3,
            grid=(1,),
            in_specs=[HBM] * len(operands),
            out_specs=HBM,
            scratch_shapes=scratch,
        ),
        compiler_params=pltpu.CompilerParams(vmem_limit_bytes=32 << 20),
        cost_estimate=pl.CostEstimate(
            flops=2 * bs**3 * pairs_hint, bytes_accessed=16 << 20, transcendentals=0
        ),
        name=f"stage{stage}",
    )(table, counts, packed, *operands)


def packed_lists(a_index, b_index, c_index, pair_count):
    position = lax.broadcasted_iota(jnp.int32, a_index.shape, 1)
    target = jnp.where(position < pair_count[:, None], c_index, SLOTS_C)
    return a_index | (b_index << B_SHIFT) | (target << C_SHIFT)


def shifted(value, axis, steps):
    count = lax.axis_size(axis)
    return lax.ppermute(value, axis, [(source, (source + steps) % count) for source in range(count)])


def any_mesh(a_blocks, b_blocks, a_index, b_index, c_index, pair_count):
    row, col = lax.axis_index("row"), lax.axis_index("col")
    rows, cols = lax.axis_size("row"), lax.axis_size("col")
    ticks = a_index.shape[2]
    back = ticks // 2 - 1
    counts = pair_count[0, 0]
    packed = packed_lists(a_index[0, 0], b_index[0, 0], c_index[0, 0], counts)
    a_now = shifted(a_blocks[0, 0], "row", back)
    b_now = shifted(b_blocks[0, 0], "col", back)
    halves = b_now.shape[0]
    running = None
    for tick in range(ticks):
        half = (row + col + tick - back) % rows // cols
        entry = jnp.concatenate(
            [jnp.array([1, tick, 0], jnp.int32), half[None].astype(jnp.int32), jnp.zeros((FIELDS - 4,), jnp.int32)]
        )
        running = run_stage(
            0, entry, counts, packed, [a_now, b_now],
            [[(0, 0, a_now.shape[0])]], [(1, h) for h in range(halves)],
            running, tick == ticks - 1, packed.shape[1],
        )
        if tick < ticks - 1:
            a_now = shifted(a_now, "row", -1)
            b_now = shifted(b_now, "col", -1)
    return running[None, None]


OWN, OUTER, INNER, SECOND, INNER_FAR, THIRD = range(6)


def b_source(col, target):
    if target == col:
        return OWN
    if col in (0, 3):
        return (None, OUTER, SECOND, THIRD)[abs(target - col)]
    if abs(target - col) == 2:
        return INNER_FAR
    return OUTER if target in (0, 3) else INNER


def stage_tables(stage_of, n_stages, rows=8, cols=4, ticks=8):
    tables = np.zeros((rows, cols, n_stages, FIELDS), np.int32)
    for row in range(rows):
        for col in range(cols):
            lists = [[] for _ in range(n_stages)]
            for tick in range(ticks):
                offset = tick - (ticks // 2 - 1)
                a_id = row ^ ((row + offset) % rows)
                source = b_source(col, (col + offset) % cols)
                half = (row + col + offset) % rows // cols
                lists[stage_of(a_id, source, half)].append((tick, a_id, 2 * source + half))
            for stage, entries in enumerate(lists):
                tables[row, col, stage, 0] = len(entries)
                for k, entry in enumerate(entries):
                    tables[row, col, stage, 1 + 3 * k : 4 + 3 * k] = entry
    return tables


def gather_b(b_own):
    outer_both, inner_both, outward = [(0, 1), (1, 0), (2, 3), (3, 2)], [(1, 2), (2, 1)], [(1, 0), (2, 3)]
    streams = []
    for half in range(2):
        own = b_own[half]
        outer = lax.ppermute(own, "col", outer_both)
        inner = lax.ppermute(own, "col", inner_both)
        second = lax.ppermute(inner, "col", outward)
        inner_far = lax.ppermute(outer, "col", inner_both)
        third = lax.ppermute(inner_far, "col", outward)
        streams.append((outer, inner, second, inner_far, third))
    return streams


def across(value, bit):
    return lax.ppermute(value, "row", [(source, source ^ bit) for source in range(8)])


def block_mesh(a_blocks, b_blocks, a_index, b_index, c_index, pair_count):
    row, col = lax.axis_index("row"), lax.axis_index("col")
    counts = pair_count[0, 0]
    packed = packed_lists(a_index[0, 0], b_index[0, 0], c_index[0, 0], counts)
    table = jnp.asarray(stage_tables(lambda a, b, h: 0, 1))[row, col].reshape(-1)
    a_own, b_own = a_blocks[0, 0], b_blocks[0, 0]
    cut = a_own.shape[0] // 2
    streams = gather_b(b_own)
    a_x, a_y = across(a_own, 2), across(a_own, 4)
    a_d = (across(a_y[:cut], 2), across(a_x[cut:], 4))
    own_chip = [a_own, a_x, a_y, *a_d]
    arrays = own_chip + [across(value, 1) for value in own_chip] + [b_own]
    slots = a_own.shape[0]
    whole = lambda number: [(number, 0, slots)]
    split = lambda number: [(number, 0, cut), (number + 1, cut, slots - cut)]
    a_views = [whole(0), whole(5), whole(1), whole(6), whole(2), whole(7), split(3), split(8)]
    b_views = [(10, 0), (10, 1)]
    for hop in range(5):
        for half in range(2):
            b_views.append((len(arrays), None))
            arrays.append(streams[half][hop])
    total = run_stage(0, table, counts, packed, arrays, a_views, b_views, None, True, 8 * packed.shape[1])
    return total[None, None]


def solution(mesh):
    placed = (
        P("row", "col", None, None, None),
        P("row", "col", None, None, None, None),
        P("row", "col", None, None),
        P("row", "col", None, None),
        P("row", "col", None, None),
        P("row", "col", None),
    )
    exact = (mesh.shape["row"], mesh.shape["col"]) == (8, 4)
    return jax.shard_map(
        block_mesh if exact else any_mesh,
        mesh=mesh,
        in_specs=placed,
        out_specs=P("row", "col", None, None, None),
        check_vma=False,
    )
```

time: 495 us -> 157 us (0.32)
  matrix products: 342 us -> 0 us
  local copies, waits for them, and re-layouts: 78.1 us -> 20.8 us
  waiting for transfers between devices: 34 us -> 78.6 us
  Pallas kernels: 0 us -> 18 us
  starting transfers between devices: 27.4 us -> 37.7 us
  other arithmetic: 6.66 us -> 0.07 us
    dot_general x40 -> x0, matrix products: 342 us -> none  [the longest x8 108 us: accumulate(): jnp.dot(placer, lower_part, preferred_element_type=jnp.float32)]
    unnamed x51 -> x46, local copies, waits for them, and re-layouts: 62.1 us -> 16 us
    ppermute x16 -> x19, waiting for transfers between devices: 34 us -> 78.6 us  [the longest x2 36.6 us: gather_b(): third = lax.ppermute(inner_far, 'col', outward)]
    pallas_call x0 -> x1, Pallas kernels: none -> 18 us  [run_stage(): pl.pallas_call(kernel, out_shape=jax.ShapeDtypeStruct((SLOTS_C, bs, bs),...]
    ppermute x16 -> x19, starting transfers between devices: 27.4 us -> 37.7 us  [the longest x2 22.3 us: gather_b(): outer = lax.ppermute(own, 'col', outer_both)]
    dynamic_slice x8 -> x0, local copies, waits for them, and re-layouts: 9.54 us -> none  [per_device(): b_panel = lax.dynamic_index_in_dim(b_current, half_index, 0, keepdims=False)]
    lt x8 -> x0, other arithmetic: 6.66 us -> none  [padded_tick(): live_mask = jnp.arange(a_list.shape[0], dtype=jnp.int32) < live_count]
  transfers between devices with their start and end apart: 16 -> 19, of which waited for: 4 -> 9; matrix products, arithmetic and copies ran while one was open for 75% -> 3% of each run, Pallas kernels for 0% -> 0%
where the time goes in v1:
time: 157 us; the launch traced here: 155 us
  waiting for transfers between devices  78.6 us (50%)
  starting transfers between devices  37.7 us (24%)
  local copies, waits for them, and re-layouts  20.8 us (13%)
  Pallas kernels  18 us (11%)
    ppermute x2, waiting for transfers between devices, gather_b(): third = lax.ppermute(inner_far, 'col', outward)  36.6 us
    ppermute x2, waiting for transfers between devices, gather_b(): second = lax.ppermute(inner, 'col', outward)  22.6 us
    ppermute x2, starting transfers between devices, gather_b(): outer = lax.ppermute(own, 'col', outer_both)  22.3 us
    pallas_call x1, Pallas kernels, run_stage(): pl.pallas_call(kernel, out_shape=jax.ShapeDtypeStruct((SLOTS_C, bs, bs),...  18 us
    unnamed x46, local copies, waits for them, and re-layouts  16 us
    ppermute x2, waiting for transfers between devices, gather_b(): outer = lax.ppermute(own, 'col', outer_both)  13.3 us
    ppermute x9, starting transfers between devices, across(): lax.ppermute(value, 'row', [(source, source ^ bit) for source in range(8)])  6.37 us
    ppermute x9, waiting for transfers between devices, across(): lax.ppermute(value, 'row', [(source, source ^ bit) for source in range(8)])  6.05 us
  transfers between devices with their start and end apart: 19, of which 9 were waited for; matrix products, arithmetic and copies ran while one was open for 3% of the time, Pallas kernels for 0%

profile of v1, /device:TPU:0, one launch (start us, length us, event | category | flops | bytes accessed | tf_op | source)
XLA Modules:
  0.0 155.4 jit_solution(7687175253315666108)
XLA Ops:
  0.0 3.0 %collective-permute-start.1 = (bf16[64,128,128]{2,1,0:T(8,128)(2,1)}, bf16[64,128,128]{2,1,0:T(8,128)(2,1)}, u32[]{:S(2)}, u32[]{:S(2)}) collective-permute-start(bf16[64,128,128]{2,1,0:T(8,128)(2,1)} %bitcast.19), channel_id=1, source_target_pairs={{0,16},{4,20},{8,24},{12,28},{16,0},{20,4},{24,8},{28,12},{1,17},{... | collective-permute-start | bytes 6291464 | tf_op jit(solution)/shard_map/ppermute | solution.py:235
  3.0 1.5 collective-permute-start
  4.5 1.5 slice_bitcast_fusion
  6.7 4.4 %collective-permute-start.10 = (bf16[24,128,128]{2,1,0:T(8,128)(2,1)S(1)}, bf16[24,128,128]{2,1,0:T(8,128)(2,1)S(1)}, u32[]{:S(2)}, u32[]{:S(2)}) collective-permute-start(bf16[24,128,128]{2,1,0:T(8,128)(2,1)S(1)} %get-tuple-element.5), channel_id=1, source_target_pairs={{0,1},{1,0},{2,3},{3,2},{4,5},{5,4},{6,7},{7,6},{8,9},{9,8},{10,11... | collective-permute-start | bytes 2359304 | tf_op jit(solution)/shard_map/ppermute | solution.py:225
  12.0 17.9 %collective-permute-start.9 = (bf16[24,128,128]{2,1,0:T(8,128)(2,1)S(1)}, bf16[24,128,128]{2,1,0:T(8,128)(2,1)S(1)}, u32[]{:S(2)}, u32[]{:S(2)}) collective-permute-start(bf16[24,128,128]{2,1,0:T(8,128)(2,1)S(1)} %get-tuple-element.6), channel_id=1, source_target_pairs={{0,1},{1,0},{2,3},{3,2},{4,5},{5,4},{6,7},{7,6},{8,9},{9,8},{10,11... | collective-permute-start | bytes 2359304 | tf_op jit(solution)/shard_map/ppermute | solution.py:225
  30.0 1.3 collective-permute-start.14
  31.3 13.3 %collective-permute-done.9.refs_11_ = bf16[24,128,128]{2,1,0:T(8,128)(2,1)S(1)} collective-permute-done((bf16[24,128,128]{2,1,0:T(8,128)(2,1)S(1)}, bf16[24,128,128]{2,1,0:T(8,128)(2,1)S(1)}, u32[]{:S(2)}, u32[]{:S(2)}) %collective-permute-start.9) | collective-permute-done | bytes 786464 | tf_op jit(solution)/shard_map/ppermute | solution.py:225
  45.4 3.6 %collective-permute-done.1.refs_2_ = bf16[64,128,128]{2,1,0:T(8,128)(2,1)} collective-permute-done((bf16[64,128,128]{2,1,0:T(8,128)(2,1)}, bf16[64,128,128]{2,1,0:T(8,128)(2,1)}, u32[]{:S(2)}, u32[]{:S(2)}) %collective-permute-start.1) | collective-permute-done | bytes 2097184 | tf_op jit(solution)/shard_map/ppermute | solution.py:235
  49.0 1.3 collective-permute-start.13
  50.4 1.5 collective-permute-start.15
  51.9 1.3 slice.18
  53.2 1.3 slice.19
  54.6 10.1 %collective-permute-done.14.refs_16_ = bf16[24,128,128]{2,1,0:T(8,128)(2,1)S(1)} collective-permute-done((bf16[24,128,128]{2,1,0:T(8,128)(2,1)S(1)}, bf16[24,128,128]{2,1,0:T(8,128)(2,1)S(1)}, u32[]{:S(2)}, u32[]{:S(2)}) %collective-permute-start.14) | collective-permute-done | bytes 786464 | tf_op jit(solution)/shard_map/ppermute | solution.py:227
  66.8 12.5 %collective-permute-done.13.refs_15_ = bf16[24,128,128]{2,1,0:T(8,128)(2,1)S(1)} collective-permute-done((bf16[24,128,128]{2,1,0:T(8,128)(2,1)S(1)}, bf16[24,128,128]{2,1,0:T(8,128)(2,1)S(1)}, u32[]{:S(2)}, u32[]{:S(2)}) %collective-permute-start.13) | collective-permute-done | bytes 786464 | tf_op jit(solution)/shard_map/ppermute | solution.py:227
  80.7 1.3 copy-done.3
  82.0 1.3 collective-permute-start.18
  84.2 2.0 %collective-permute-done.2.refs_3_ = bf16[32,128,128]{2,1,0:T(8,128)(2,1)S(1)} collective-permute-done((bf16[32,128,128]{2,1,0:T(8,128)(2,1)S(1)}, bf16[32,128,128]{2,1,0:T(8,128)(2,1)S(1)}, u32[]{:S(2)}, u32[]{:S(2)}) %collective-permute-start.2) | collective-permute-done | bytes 1048608 | tf_op jit(solution)/shard_map/ppermute | solution.py:235
  86.7 17.2 %collective-permute-done.18.refs_20_ = bf16[24,128,128]{2,1,0:T(8,128)(2,1)S(1)} collective-permute-done((bf16[24,128,128]{2,1,0:T(8,128)(2,1)S(1)}, bf16[24,128,128]{2,1,0:T(8,128)(2,1)S(1)}, u32[]{:S(2)}, u32[]{:S(2)}) %collective-permute-start.18) | collective-permute-done | bytes 786464 | tf_op jit(solution)/shard_map/ppermute | solution.py:229
  104.8 1.3 collective-permute-start.17
  106.9 19.4 %collective-permute-done.17.refs_19_ = bf16[24,128,128]{2,1,0:T(8,128)(2,1)} collective-permute-done((bf16[24,128,128]{2,1,0:T(8,128)(2,1)}, bf16[24,128,128]{2,1,0:T(8,128)(2,1)}, u32[]{:S(2)}, u32[]{:S(2)}) %collective-permute-start.17) | collective-permute-done | bytes 786464 | tf_op jit(solution)/shard_map/ppermute | solution.py:229
  126.3 1.6 %copy-done.2 = bf16[1,1,64,128,128]{4,3,2,1,0:T(8,128)(2,1)S(1)} copy-done((bf16[1,1,64,128,128]{4,3,2,1,0:T(8,128)(2,1)S(1)}, bf16[1,1,64,128,128]{4,3,2,1,0:T(8,128)(2,1)}, u32[]{:S(2)}) %copy-start.2) | copy-done | bytes 2097176
  127.9 1.6 %copy-done.4 = bf16[64,128,128]{2,1,0:T(8,128)(2,1)S(1)} copy-done((bf16[64,128,128]{2,1,0:T(8,128)(2,1)S(1)}, bf16[64,128,128]{2,1,0:T(8,128)(2,1)}, u32[]{:S(2)}) %copy-start.4) | copy-done | bytes 2097176
  130.6 1.1 copy-done.8
  137.4 18.0 %stage0.1 = bf16[64,128,128]{2,1,0:T(8,128)(2,1)} custom-call(s32[32]{0:T(128)S(1)} %dynamic-slice_bitcast_fusion.table, s32[8]{0:T(128)S(1)} %bitcast.24, s32[8,192]{1,0:T(8,128)S(1)} %fusion.1.packed, bf16[64,128,128]{2,1,0:T(8,128)(2,1)S(1)} %bitcast.22, bf16[64,128,128]{2,1,0:T(8,128)(2,1)} %collective-permute-done.refs_1_, ...), custom_call_target="tpu_custom_call" | custom-call | flops 6442450944 | bytes 16777216 | tf_op jit(solution)/shard_map/stage0/pallas_call | solution.py:133
  (66 shorter events, 15.8 us)
Async XLA Ops:
  0.0 49.0 %collective-permute-start.1 = (bf16[64,128,128]{2,1,0:T(8,128)(2,1)}, bf16[64,128,128]{2,1,0:T(8,128)(2,1)}, u32[]{:S(2)}, u32[]{:S(2)}) collective-permute-start(bf16[64,128,128]{2,1,0:T(8,128)(2,1)} %bitcast.19), channel_id=1, source_target_pairs={{0,16},{4,20},{8,24},{12,28},{16,0},{20,4},{24,8},{28,12},{1,17},{... | collective-permute-start | bytes 6291464 | tf_op jit(solution)/shard_map/ppermute | solution.py:235
  3.0 47.4 %collective-permute-start = (bf16[64,128,128]{2,1,0:T(8,128)(2,1)}, bf16[64,128,128]{2,1,0:T(8,128)(2,1)}, u32[]{:S(2)}, u32[]{:S(2)}) collective-permute-start(bf16[64,128,128]{2,1,0:T(8,128)(2,1)} %bitcast.20), channel_id=1, source_target_pairs={{0,8},{4,12},{8,0},{12,4},{16,24},{20,28},{24,16},{28,20},{1,9},{5... | collective-permute-start | bytes 6291464 | tf_op jit(solution)/shard_map/ppermute | solution.py:235
  6.0 6.0 %collective-permute-start.12 = (bf16[24,128,128]{2,1,0:T(8,128)(2,1)S(1)}, bf16[24,128,128]{2,1,0:T(8,128)(2,1)S(1)}, u32[]{:S(2)}, u32[]{:S(2)}) collective-permute-start(bf16[24,128,128]{2,1,0:T(8,128)(2,1)S(1)} %get-tuple-element.5), channel_id=1, source_target_pairs={{1,2},{2,1},{5,6},{6,5},{9,10},{10,9},{13,14},{14,13},{17,18},{18,... | collective-permute-start | bytes 2359304 | tf_op jit(solution)/shard_map/ppermute | solution.py:226
  6.7 23.2 %collective-permute-start.10 = (bf16[24,128,128]{2,1,0:T(8,128)(2,1)S(1)}, bf16[24,128,128]{2,1,0:T(8,128)(2,1)S(1)}, u32[]{:S(2)}, u32[]{:S(2)}) collective-permute-start(bf16[24,128,128]{2,1,0:T(8,128)(2,1)S(1)} %get-tuple-element.5), channel_id=1, source_target_pairs={{0,1},{1,0},{2,3},{3,2},{4,5},{5,4},{6,7},{7,6},{8,9},{9,8},{10,11... | collective-permute-start | bytes 2359304 | tf_op jit(solution)/shard_map/ppermute | solution.py:225
  11.1 95.7 %copy-start.19 = (s32[1,1,8]{2,1,0:T(1,128)S(1)}, s32[1,1,8]{2,1,0:T(1,128)}, u32[]{:S(2)}) copy-start(s32[1,1,8]{2,1,0:T(1,128)} %param.12) | copy-start | bytes 100
  11.1 95.7 %copy-start.20 = (s32[1,1,8,192]{3,2,1,0:T(8,128)S(1)}, s32[1,1,8,192]{3,2,1,0:T(8,128)}, u32[]{:S(2)}) copy-start(s32[1,1,8,192]{3,2,1,0:T(8,128)} %param.11) | copy-start | bytes 18436
  11.1 95.7 %copy-start.21 = (s32[1,1,8,192]{3,2,1,0:T(8,128)S(1)}, s32[1,1,8,192]{3,2,1,0:T(8,128)}, u32[]{:S(2)}) copy-start(s32[1,1,8,192]{3,2,1,0:T(8,128)} %param.9) | copy-start | bytes 18436
  11.1 95.7 %copy-start.22 = (s32[1,1,8,192]{3,2,1,0:T(8,128)S(1)}, s32[1,1,8,192]{3,2,1,0:T(8,128)}, u32[]{:S(2)}) copy-start(s32[1,1,8,192]{3,2,1,0:T(8,128)} %param.10) | copy-start | bytes 18436
  11.1 115.2 %copy-start = (bf16[1,1,2,24,128,128]{5,4,3,2,1,0:T(8,128)(2,1)S(1)}, bf16[1,1,2,24,128,128]{5,4,3,2,1,0:T(8,128)(2,1)}, u32[]{:S(2)}) copy-start(bf16[1,1,2,24,128,128]{5,4,3,2,1,0:T(8,128)(2,1)} %param.8) | copy-start | bytes 4718596
  11.1 18.9 %collective-permute-start.11 = (bf16[24,128,128]{2,1,0:T(8,128)(2,1)S(1)}, bf16[24,128,128]{2,1,0:T(8,128)(2,1)S(1)}, u32[]{:S(2)}, u32[]{:S(2)}) collective-permute-start(bf16[24,128,128]{2,1,0:T(8,128)(2,1)S(1)} %get-tuple-element.6), channel_id=1, source_target_pairs={{1,2},{2,1},{5,6},{6,5},{9,10},{10,9},{13,14},{14,13},{17,18},{18,... | collective-permute-start | bytes 2359304 | tf_op jit(solution)/shard_map/ppermute | solution.py:226
  12.0 32.7 %collective-permute-start.9 = (bf16[24,128,128]{2,1,0:T(8,128)(2,1)S(1)}, bf16[24,128,128]{2,1,0:T(8,128)(2,1)S(1)}, u32[]{:S(2)}, u32[]{:S(2)}) collective-permute-start(bf16[24,128,128]{2,1,0:T(8,128)(2,1)S(1)} %get-tuple-element.6), channel_id=1, source_target_pairs={{0,1},{1,0},{2,3},{3,2},{4,5},{5,4},{6,7},{7,6},{8,9},{9,8},{10,11... | collective-permute-start | bytes 2359304 | tf_op jit(solution)/shard_map/ppermute | solution.py:225
  29.9 50.8 %collective-permute-start.4 = (bf16[64,128,128]{2,1,0:T(8,128)(2,1)S(1)}, bf16[64,128,128]{2,1,0:T(8,128)(2,1)S(1)}, u32[]{:S(2)}, u32[]{:S(2)}) collective-permute-start(bf16[64,128,128]{2,1,0:T(8,128)(2,1)S(1)} %bitcast.21), channel_id=1, source_target_pairs={{0,4},{4,0},{8,12},{12,8},{16,20},{20,16},{24,28},{28,24},{1,5},{5... | collective-permute-start | bytes 6291464 | tf_op jit(solution)/shard_map/ppermute | solution.py:235
  30.0 34.7 %collective-permute-start.14 = (bf16[24,128,128]{2,1,0:T(8,128)(2,1)S(1)}, bf16[24,128,128]{2,1,0:T(8,128)(2,1)S(1)}, u32[]{:S(2)}, u32[]{:S(2)}) collective-permute-start(bf16[24,128,128]{2,1,0:T(8,128)(2,1)S(1)} %collective-permute-done.12.refs_14_), channel_id=1, source_target_pairs={{1,0},{2,3},{5,4},{6,7},{9,8},{10,11},{13,12},{14,15},{17,16},{18,... | collective-permute-start | bytes 2359304 | tf_op jit(solution)/shard_map/ppermute | solution.py:227
  44.7 21.5 %collective-permute-start.16 = (bf16[24,128,128]{2,1,0:T(8,128)(2,1)S(1)}, bf16[24,128,128]{2,1,0:T(8,128)(2,1)S(1)}, u32[]{:S(2)}, u32[]{:S(2)}) collective-permute-start(bf16[24,128,128]{2,1,0:T(8,128)(2,1)S(1)} %collective-permute-done.10.refs_12_), channel_id=1, source_target_pairs={{1,2},{2,1},{5,6},{6,5},{9,10},{10,9},{13,14},{14,13},{17,18},{18,... | collective-permute-start | bytes 2359304 | tf_op jit(solution)/shard_map/ppermute | solution.py:228
  49.0 30.3 %collective-permute-start.13 = (bf16[24,128,128]{2,1,0:T(8,128)(2,1)S(1)}, bf16[24,128,128]{2,1,0:T(8,128)(2,1)S(1)}, u32[]{:S(2)}, u32[]{:S(2)}) collective-permute-start(bf16[24,128,128]{2,1,0:T(8,128)(2,1)S(1)} %collective-permute-done.11.refs_13_), channel_id=1, source_target_pairs={{1,0},{2,3},{5,4},{6,7},{9,8},{10,11},{13,12},{14,15},{17,16},{18,... | collective-permute-start | bytes 2359304 | tf_op jit(solution)/shard_map/ppermute | solution.py:227
  50.4 29.8 %collective-permute-start.15 = (bf16[24,128,128]{2,1,0:T(8,128)(2,1)S(1)}, bf16[24,128,128]{2,1,0:T(8,128)(2,1)}, u32[]{:S(2)}, u32[]{:S(2)}) collective-permute-start(bf16[24,128,128]{2,1,0:T(8,128)(2,1)S(1)} %collective-permute-done.9.refs_11_), channel_id=1, source_target_pairs={{1,2},{2,1},{5,6},{6,5},{9,10},{10,9},{13,14},{14,13},{17,18},{18,... | collective-permute-start | bytes 2359304 | tf_op jit(solution)/shard_map/ppermute | solution.py:228
  65.6 20.6 %collective-permute-start.2 = (bf16[32,128,128]{2,1,0:T(8,128)(2,1)S(1)}, bf16[32,128,128]{2,1,0:T(8,128)(2,1)S(1)}, u32[]{:S(2)}, u32[]{:S(2)}) collective-permute-start(bf16[32,128,128]{2,1,0:T(8,128)(2,1)S(1)} %slice.18), channel_id=1, source_target_pairs={{0,8},{4,12},{8,0},{12,4},{16,24},{20,28},{24,16},{28,20},{1,9},{5... | collective-permute-start | bytes 3145736 | tf_op jit(solution)/shard_map/ppermute | solution.py:235
  66.2 20.4 %collective-permute-start.3 = (bf16[32,128,128]{2,1,0:T(8,128)(2,1)S(1)}, bf16[32,128,128]{2,1,0:T(8,128)(2,1)}, u32[]{:S(2)}, u32[]{:S(2)}) collective-permute-start(bf16[32,128,128]{2,1,0:T(8,128)(2,1)S(1)} %slice.19), channel_id=1, source_target_pairs={{0,16},{4,20},{8,24},{12,28},{16,0},{20,4},{24,8},{28,12},{1,17},{... | collective-permute-start | bytes 3145736 | tf_op jit(solution)/shard_map/ppermute | solution.py:235
  80.2 46.1 %collective-permute-start.6 = (bf16[64,128,128]{2,1,0:T(8,128)(2,1)}, bf16[64,128,128]{2,1,0:T(8,128)(2,1)}, u32[]{:S(2)}, u32[]{:S(2)}) collective-permute-start(bf16[64,128,128]{2,1,0:T(8,128)(2,1)} %collective-permute-done.1.refs_2_), channel_id=1, source_target_pairs={{0,4},{4,0},{8,12},{12,8},{16,20},{20,16},{24,28},{28,24},{1,5},{5... | collective-permute-start | bytes 6291464 | tf_op jit(solution)/shard_map/ppermute | solution.py:235
  80.2 46.1 %collective-permute-start.5 = (bf16[64,128,128]{2,1,0:T(8,128)(2,1)}, bf16[64,128,128]{2,1,0:T(8,128)(2,1)}, u32[]{:S(2)}, u32[]{:S(2)}) collective-permute-start(bf16[64,128,128]{2,1,0:T(8,128)(2,1)} %collective-permute-done.refs_1_), channel_id=1, source_target_pairs={{0,4},{4,0},{8,12},{12,8},{16,20},{20,16},{24,28},{28,24},{1,5},{5... | collective-permute-start | bytes 6291464 | tf_op jit(solution)/shard_map/ppermute | solution.py:235
  82.0 21.9 %collective-permute-start.18 = (bf16[24,128,128]{2,1,0:T(8,128)(2,1)S(1)}, bf16[24,128,128]{2,1,0:T(8,128)(2,1)S(1)}, u32[]{:S(2)}, u32[]{:S(2)}) collective-permute-start(bf16[24,128,128]{2,1,0:T(8,128)(2,1)S(1)} %collective-permute-done.16.refs_18_), channel_id=1, source_target_pairs={{1,0},{2,3},{5,4},{6,7},{9,8},{10,11},{13,12},{14,15},{17,16},{18,... | collective-permute-start | bytes 2359304 | tf_op jit(solution)/shard_map/ppermute | solution.py:229
  86.2 40.1 %collective-permute-start.7 = (bf16[32,128,128]{2,1,0:T(8,128)(2,1)S(1)}, bf16[32,128,128]{2,1,0:T(8,128)(2,1)}, u32[]{:S(2)}, u32[]{:S(2)}) collective-permute-start(bf16[32,128,128]{2,1,0:T(8,128)(2,1)S(1)} %collective-permute-done.2.refs_3_), channel_id=1, source_target_pairs={{0,4},{4,0},{8,12},{12,8},{16,20},{20,16},{24,28},{28,24},{1,5},{5... | collective-permute-start | bytes 3145736 | tf_op jit(solution)/shard_map/ppermute | solution.py:235
  86.6 39.7 %collective-permute-start.8 = (bf16[32,128,128]{2,1,0:T(8,128)(2,1)}, bf16[32,128,128]{2,1,0:T(8,128)(2,1)}, u32[]{:S(2)}, u32[]{:S(2)}) collective-permute-start(bf16[32,128,128]{2,1,0:T(8,128)(2,1)} %collective-permute-done.3.refs_4_), channel_id=1, source_target_pairs={{0,4},{4,0},{8,12},{12,8},{16,20},{20,16},{24,28},{28,24},{1,5},{5... | collective-permute-start | bytes 3145736 | tf_op jit(solution)/shard_map/ppermute | solution.py:235
  104.8 21.5 %collective-permute-start.17 = (bf16[24,128,128]{2,1,0:T(8,128)(2,1)}, bf16[24,128,128]{2,1,0:T(8,128)(2,1)}, u32[]{:S(2)}, u32[]{:S(2)}) collective-permute-start(bf16[24,128,128]{2,1,0:T(8,128)(2,1)} %collective-permute-done.15.refs_17_), channel_id=1, source_target_pairs={{1,0},{2,3},{5,4},{6,7},{9,8},{10,11},{13,12},{14,15},{17,16},{18,... | collective-permute-start | bytes 2359304 | tf_op jit(solution)/shard_map/ppermute | solution.py:229
  (18 other events, 105.1 us)

commit v2 on v1

--- a/solution.py
+++ b/solution.py
@@ -28,16 +28,16 @@
     def fetch(k, slot):
         a_id = table[base + 2 + 3 * k]
         b_id = table[base + 3 + 3 * k]
-        for number, pieces in enumerate(a_views):
+        for number, pieces in a_views.items():
 
             @pl.when(a_id == number)
             def _(pieces=pieces):
-                for ref_number, offset, size in pieces:
-                    pltpu.make_async_copy(
-                        inputs[ref_number], a_buf.at[slot, pl.ds(offset, size)], a_sem.at[slot]
-                    ).start()
-
-        for number, (ref_number, half) in enumerate(b_views):
+                size = a_buf.shape[1] // len(pieces)
+                for piece, ref_number in enumerate(pieces):
+                    target = a_buf.at[slot, pl.ds(piece * size, size)]
+                    pltpu.make_async_copy(inputs[ref_number], target, a_sem.at[slot]).start()
+
+        for number, (ref_number, half) in b_views.items():
 
             @pl.when(b_id == number)
             def _(ref_number=ref_number, half=half):
@@ -107,8 +107,8 @@
 
 def run_stage(stage, table, counts, packed, arrays, a_views, b_views, c_in, last, pairs_hint):
     first = c_in is None
-    slots_a = max(sum(piece[2] for piece in pieces) for pieces in a_views)
-    slots_b, bs = arrays[b_views[0][0]].shape[-3:-1]
+    slots_a = sum(arrays[number].shape[0] for number in next(iter(a_views.values())))
+    slots_b, bs = arrays[next(iter(b_views.values()))[0]].shape[-3:-1]
     operands = list(arrays) + ([] if first else [c_in])
     kernel = functools.partial(
         stage_kernel,
@@ -140,9 +140,9 @@
             out_specs=HBM,
             scratch_shapes=scratch,
         ),
-        compiler_params=pltpu.CompilerParams(vmem_limit_bytes=32 << 20),
+        compiler_params=pltpu.CompilerParams(vmem_limit_bytes=60 << 20),
         cost_estimate=pl.CostEstimate(
-            flops=2 * bs**3 * pairs_hint, bytes_accessed=16 << 20, transcendentals=0
+            flops=0, bytes_accessed=0, transcendentals=0
         ),
         name=f"stage{stage}",
     )(table, counts, packed, *operands)
@@ -177,7 +177,7 @@
         )
         running = run_stage(
             0, entry, counts, packed, [a_now, b_now],
-            [[(0, 0, a_now.shape[0])]], [(1, h) for h in range(halves)],
+            {0: (0,)}, {h: (1, h) for h in range(halves)},
             running, tick == ticks - 1, packed.shape[1],
         )
         if tick < ticks - 1:
@@ -186,7 +186,15 @@
     return running[None, None]
 
 
+ROWS, COLS = 8, 4
 OWN, OUTER, INNER, SECOND, INNER_FAR, THIRD = range(6)
+A_STAGE = (0, 0, 0, 0, 0, 0, 0, 0)
+B_STAGE = ((0, 0), (0, 0), (0, 0), (0, 0), (0, 0), (0, 1))
+STAGES = 2
+
+
+def a_place(row, target):
+    return row ^ target
 
 
 def b_source(col, target):
@@ -199,17 +207,18 @@
     return OUTER if target in (0, 3) else INNER
 
 
-def stage_tables(stage_of, n_stages, rows=8, cols=4, ticks=8):
-    tables = np.zeros((rows, cols, n_stages, FIELDS), np.int32)
-    for row in range(rows):
-        for col in range(cols):
-            lists = [[] for _ in range(n_stages)]
+def stage_tables(ticks=8):
+    tables = np.zeros((ROWS, COLS, STAGES, FIELDS), np.int32)
+    for row in range(ROWS):
+        for col in range(COLS):
+            lists = [[] for _ in range(STAGES)]
             for tick in range(ticks):
                 offset = tick - (ticks // 2 - 1)
-                a_id = row ^ ((row + offset) % rows)
-                source = b_source(col, (col + offset) % cols)
-                half = (row + col + offset) % rows // cols
-                lists[stage_of(a_id, source, half)].append((tick, a_id, 2 * source + half))
+                place = a_place(row, (row + offset) % ROWS)
+                source = b_source(col, (col + offset) % COLS)
+                half = (row + col + offset) % ROWS // COLS
+                ready = max(A_STAGE[place], B_STAGE[source][half])
+                lists[ready].append((tick, place, 2 * source + half))
             for stage, entries in enumerate(lists):
                 tables[row, col, stage, 0] = len(entries)
                 for k, entry in enumerate(entries):
@@ -217,46 +226,96 @@
     return tables
 
 
-def gather_b(b_own):
-    outer_both, inner_both, outward = [(0, 1), (1, 0), (2, 3), (3, 2)], [(1, 2), (2, 1)], [(1, 0), (2, 3)]
-    streams = []
-    for half in range(2):
-        own = b_own[half]
-        outer = lax.ppermute(own, "col", outer_both)
-        inner = lax.ppermute(own, "col", inner_both)
-        second = lax.ppermute(inner, "col", outward)
-        inner_far = lax.ppermute(outer, "col", inner_both)
-        third = lax.ppermute(inner_far, "col", outward)
-        streams.append((outer, inner, second, inner_far, third))
-    return streams
-
-
-def across(value, bit):
-    return lax.ppermute(value, "row", [(source, source ^ bit) for source in range(8)])
+def used(tables, stage, field):
+    found = set()
+    for entries in tables[:, :, stage].reshape(-1, FIELDS):
+        found |= {int(entries[field + 3 * k]) for k in range(entries[0])}
+    return sorted(found)
+
+
+def sent(name, value, place_of):
+    pairs = []
+    for row in range(ROWS):
+        for col in range(COLS):
+            to_row, to_col = place_of(row, col)
+            pairs.append((COLS * row + col, COLS * to_row + to_col))
+    with jax.named_scope(name):
+        return lax.ppermute(value, ("row", "col"), pairs)
+
+
+def after(value, *others):
+    return lax.optimization_barrier((value, *others))[0]
+
+
+def outward(value, name):
+    return sent(name, value, lambda row, col: (row, col ^ 1))
+
+
+def inward(value, name):
+    return sent(name, value, lambda row, col: (row, 3 - col) if col in (1, 2) else (row ^ 1, col))
+
+
+def second_over(value, name):
+    return sent(name, value, lambda row, col: (row ^ 1, (2, 0, 3, 1)[col]) if col in (0, 3) else (row, (2, 0, 3, 1)[col]))
+
+
+def end_to_end(value, name):
+    return sent(name, value, lambda row, col: (row, 3 - col) if col in (0, 3) else (row ^ 1, col))
+
+
+def swapped(value, name):
+    return sent(name, value, lambda row, col: (row ^ 1, col))
+
+
+def across(value, bits, name):
+    return sent(name, value, lambda row, col: (row ^ bits, col))
 
 
 def block_mesh(a_blocks, b_blocks, a_index, b_index, c_index, pair_count):
     row, col = lax.axis_index("row"), lax.axis_index("col")
     counts = pair_count[0, 0]
     packed = packed_lists(a_index[0, 0], b_index[0, 0], c_index[0, 0], counts)
-    table = jnp.asarray(stage_tables(lambda a, b, h: 0, 1))[row, col].reshape(-1)
+    tables = stage_tables(a_index.shape[2])
+    table = jnp.asarray(tables)[row, col].reshape(-1)
     a_own, b_own = a_blocks[0, 0], b_blocks[0, 0]
+    def stage_call(stage, total):
+        arrays, a_views, b_views = [], {}, {}
+
+        def number_of(value):
+            for number, held in enumerate(arrays):
+                if held is value:
+                    return number
+            arrays.append(value)
+            return len(arrays) - 1
+
+        for place in used(tables, stage, 2):
+            a_views[place] = tuple(number_of(value) for value in a_at[place])
+        for source in used(tables, stage, 3):
+            value, half = b_at[source]
+            b_views[source] = (number_of(value), half)
+        return run_stage(stage, table, counts, packed, arrays, a_views, b_views, total, stage == STAGES - 1, 150)
+
+    outer, inner, second_b, inner_far, third = [], [], [], [], []
+    by_x, by_y = across(a_own, 2, "Ax"), across(a_own, 4, "Ay")
     cut = a_own.shape[0] // 2
-    streams = gather_b(b_own)
-    a_x, a_y = across(a_own, 2), across(a_own, 4)
-    a_d = (across(a_y[:cut], 2), across(a_x[cut:], 4))
-    own_chip = [a_own, a_x, a_y, *a_d]
-    arrays = own_chip + [across(value, 1) for value in own_chip] + [b_own]
-    slots = a_own.shape[0]
-    whole = lambda number: [(number, 0, slots)]
-    split = lambda number: [(number, 0, cut), (number + 1, cut, slots - cut)]
-    a_views = [whole(0), whole(5), whole(1), whole(6), whole(2), whole(7), split(3), split(8)]
-    b_views = [(10, 0), (10, 1)]
-    for hop in range(5):
-        for half in range(2):
-            b_views.append((len(arrays), None))
-            arrays.append(streams[half][hop])
-    total = run_stage(0, table, counts, packed, arrays, a_views, b_views, None, True, 8 * packed.shape[1])
+    for half in range(2):
+        outer.append(outward(b_own[half], f"O{half}"))
+        inner.append(inward(b_own[half], f"I{half}"))
+        second_b.append(outward(inner[half], f"S{half}"))
+        inner_far.append(inward(outer[half], f"F{half}"))
+        third.append(outward(inner_far[half], f"T{half}"))
+    by_both = (across(by_y[:cut], 2, "Ad0"), across(by_x[cut:], 4, "Ad1"))
+    on_chip = [(a_own,), (by_x,), (by_y,), by_both]
+    a_at = []
+    for number, pieces in enumerate(on_chip):
+        a_at += [pieces, tuple(swapped(value, f"W{number}") for value in pieces)]
+    b_at = [(b_own, 0), (b_own, 1)]
+    for halves in (outer, inner, second_b, inner_far, third):
+        b_at += [(value, None) for value in halves]
+    total = None
+    for stage in range(STAGES):
+        total = stage_call(stage, total)
+
     return total[None, None]
 
 
@@ -269,7 +328,7 @@
         P("row", "col", None, None),
         P("row", "col", None),
     )
-    exact = (mesh.shape["row"], mesh.shape["col"]) == (8, 4)
+    exact = (mesh.shape["row"], mesh.shape["col"]) == (ROWS, COLS)
     return jax.shard_map(
         block_mesh if exact else any_mesh,
         mesh=mesh,

time: 157 us -> 137 us (0.87)
  the two profiles are of different devices: /device:TPU:0 before, /device:TPU:1 now
where the time goes in v2:
time: 137 us; the launch traced here: 135 us
  waiting for transfers between devices  75 us (55%)
  Pallas kernels  26.9 us (20%)
  starting transfers between devices  25.6 us (19%)
  local copies, waits for them, and re-layouts  6.42 us (5%)
    ppermute x19, waiting for transfers between devices, sent(): return lax.ppermute(value, ('row', 'col'), pairs)  75 us
    pallas_call x2, Pallas kernels, run_stage(): pl.pallas_call(kernel, out_shape=jax.ShapeDtypeStruct((SLOTS_C, bs, bs),...  26.9 us
    ppermute x19, starting transfers between devices, sent(): return lax.ppermute(value, ('row', 'col'), pairs)  25.6 us
  transfers between devices with their start and end apart: 19, of which 6 were waited for; matrix products, arithmetic and copies ran while one was open for 5% of the time, Pallas kernels for 16%

profile of v2, /device:TPU:1, one launch (start us, length us, event | category | flops | bytes accessed | tf_op | source)
XLA Modules:
  0.0 134.7 jit_solution(8366071271398594527)
XLA Ops:
  0.0 2.1 %collective-permute-start.3 = (bf16[64,128,128]{2,1,0:T(8,128)(2,1)}, bf16[64,128,128]{2,1,0:T(8,128)(2,1)}, u32[]{:S(2)}, u32[]{:S(2)}) collective-permute-start(bf16[64,128,128]{2,1,0:T(8,128)(2,1)} %bitcast.17), channel_id=1, source_target_pairs={{0,16},{1,17},{2,18},{3,19},{4,20},{5,21},{6,22},{7,23},{8,24},{9,... | collective-permute-start | bytes 6291464 | tf_op jit(solution)/shard_map/Ay/ppermute | solution.py:243
  2.1 1.2 collective-permute-start.1
  3.3 1.5 %slice_bitcast_fusion = (bf16[24,128,128]{2,1,0:T(8,128)(2,1)S(1)}, bf16[24,128,128]{2,1,0:T(8,128)(2,1)S(1)}) fusion(bf16[1,1,2,24,128,128]{5,4,3,2,1,0:T(8,128)(2,1)} %param.8), kind=kLoop, calls=%fused_computation | loop fusion | bytes 3145728 | tf_op jit(solution)/shard_map/squeeze | solution.py:302
  4.8 1.4 %collective-permute-start.12 = (bf16[24,128,128]{2,1,0:T(8,128)(2,1)S(1)}, bf16[24,128,128]{2,1,0:T(8,128)(2,1)S(1)}, u32[]{:S(2)}, u32[]{:S(2)}) collective-permute-start(bf16[24,128,128]{2,1,0:T(8,128)(2,1)S(1)} %get-tuple-element.5), channel_id=1, source_target_pairs={{0,1},{1,0},{2,3},{3,2},{4,5},{5,4},{6,7},{7,6},{8,9},{9,8},{10,11... | collective-permute-start | bytes 2359304 | tf_op jit(solution)/shard_map/O0/ppermute | solution.py:243
  6.4 1.8 %collective-permute-start.13 = (bf16[24,128,128]{2,1,0:T(8,128)(2,1)S(1)}, bf16[24,128,128]{2,1,0:T(8,128)(2,1)S(1)}, u32[]{:S(2)}, u32[]{:S(2)}) collective-permute-start(bf16[24,128,128]{2,1,0:T(8,128)(2,1)S(1)} %get-tuple-element.5), channel_id=1, source_target_pairs={{0,4},{1,2},{2,1},{3,7},{4,0},{5,6},{6,5},{7,3},{8,12},{9,10},{10,... | collective-permute-start | bytes 2359304 | tf_op jit(solution)/shard_map/I0/ppermute | solution.py:243
  8.2 14.6 %collective-permute-done.12.refs_11_ = bf16[24,128,128]{2,1,0:T(8,128)(2,1)S(1)} collective-permute-done((bf16[24,128,128]{2,1,0:T(8,128)(2,1)S(1)}, bf16[24,128,128]{2,1,0:T(8,128)(2,1)S(1)}, u32[]{:S(2)}, u32[]{:S(2)}) %collective-permute-start.12) | collective-permute-done | bytes 786464 | tf_op jit(solution)/shard_map/O0/ppermute | solution.py:243
  22.8 3.8 %collective-permute-start.14 = (bf16[24,128,128]{2,1,0:T(8,128)(2,1)S(1)}, bf16[24,128,128]{2,1,0:T(8,128)(2,1)S(1)}, u32[]{:S(2)}, u32[]{:S(2)}) collective-permute-start(bf16[24,128,128]{2,1,0:T(8,128)(2,1)S(1)} %get-tuple-element.6), channel_id=1, source_target_pairs={{0,4},{1,2},{2,1},{3,7},{4,0},{5,6},{6,5},{7,3},{8,12},{9,10},{10,... | collective-permute-start | bytes 2359304 | tf_op jit(solution)/shard_map/I1/ppermute | solution.py:243
  26.6 13.0 %collective-permute-done.9.refs_12_ = bf16[24,128,128]{2,1,0:T(8,128)(2,1)S(1)} collective-permute-done((bf16[24,128,128]{2,1,0:T(8,128)(2,1)S(1)}, bf16[24,128,128]{2,1,0:T(8,128)(2,1)S(1)}, u32[]{:S(2)}, u32[]{:S(2)}) %collective-permute-start.9) | collective-permute-done | bytes 786464 | tf_op jit(solution)/shard_map/O1/ppermute | solution.py:243
  39.7 2.1 %collective-permute-start = (bf16[64,128,128]{2,1,0:T(8,128)(2,1)S(1)}, bf16[64,128,128]{2,1,0:T(8,128)(2,1)S(1)}, u32[]{:S(2)}, u32[]{:S(2)}) collective-permute-start(bf16[64,128,128]{2,1,0:T(8,128)(2,1)S(1)} %bitcast.20), channel_id=1, source_target_pairs={{0,4},{1,5},{2,6},{3,7},{4,0},{5,1},{6,2},{7,3},{8,12},{9,13},{10,... | collective-permute-start | bytes 6291464 | tf_op jit(solution)/shard_map/W0/ppermute | solution.py:243
  42.2 5.6 %collective-permute-done.3.refs_4_ = bf16[64,128,128]{2,1,0:T(8,128)(2,1)} collective-permute-done((bf16[64,128,128]{2,1,0:T(8,128)(2,1)}, bf16[64,128,128]{2,1,0:T(8,128)(2,1)}, u32[]{:S(2)}, u32[]{:S(2)}) %collective-permute-start.3) | collective-permute-done | bytes 2097184 | tf_op jit(solution)/shard_map/Ay/ppermute | solution.py:243
  47.8 1.1 collective-permute-start.15
  49.9 1.3 slice.20
  51.2 1.3 slice.21
  52.6 1.3 collective-permute-start.5
  54.3 11.4 %collective-permute-done.15.refs_15_ = bf16[24,128,128]{2,1,0:T(8,128)(2,1)S(1)} collective-permute-done((bf16[24,128,128]{2,1,0:T(8,128)(2,1)S(1)}, bf16[24,128,128]{2,1,0:T(8,128)(2,1)S(1)}, u32[]{:S(2)}, u32[]{:S(2)}) %collective-permute-start.15) | collective-permute-done | bytes 786464 | tf_op jit(solution)/shard_map/S0/ppermute | solution.py:243
  65.7 3.8 %collective-permute-start.2 = (bf16[64,128,128]{2,1,0:T(8,128)(2,1)}, bf16[64,128,128]{2,1,0:T(8,128)(2,1)}, u32[]{:S(2)}, u32[]{:S(2)}) collective-permute-start(bf16[64,128,128]{2,1,0:T(8,128)(2,1)} %collective-permute-done.1.refs_2_), channel_id=1, source_target_pairs={{0,4},{1,5},{2,6},{3,7},{4,0},{5,1},{6,2},{7,3},{8,12},{9,13},{10,... | collective-permute-start | bytes 6291464 | tf_op jit(solution)/shard_map/W1/ppermute | solution.py:243
  69.5 12.9 %collective-permute-done.16.refs_16_ = bf16[24,128,128]{2,1,0:T(8,128)(2,1)S(1)} collective-permute-done((bf16[24,128,128]{2,1,0:T(8,128)(2,1)S(1)}, bf16[24,128,128]{2,1,0:T(8,128)(2,1)S(1)}, u32[]{:S(2)}, u32[]{:S(2)}) %collective-permute-start.16) | collective-permute-done | bytes 786464 | tf_op jit(solution)/shard_map/S1/ppermute | solution.py:243
  82.5 2.1 %collective-permute-start.4 = (bf16[64,128,128]{2,1,0:T(8,128)(2,1)}, bf16[64,128,128]{2,1,0:T(8,128)(2,1)}, u32[]{:S(2)}, u32[]{:S(2)}) collective-permute-start(bf16[64,128,128]{2,1,0:T(8,128)(2,1)} %collective-permute-done.3.refs_4_), channel_id=1, source_target_pairs={{0,4},{1,5},{2,6},{3,7},{4,0},{5,1},{6,2},{7,3},{8,12},{9,13},{10,... | collective-permute-start | bytes 6291464 | tf_op jit(solution)/shard_map/W2/ppermute | solution.py:243
  84.6 1.1 collective-permute-start.18
  86.3 17.5 %collective-permute-done.18.refs_19_ = bf16[24,128,128]{2,1,0:T(8,128)(2,1)S(1)} collective-permute-done((bf16[24,128,128]{2,1,0:T(8,128)(2,1)S(1)}, bf16[24,128,128]{2,1,0:T(8,128)(2,1)S(1)}, u32[]{:S(2)}, u32[]{:S(2)}) %collective-permute-start.18) | collective-permute-done | bytes 786464 | tf_op jit(solution)/shard_map/T0/ppermute | solution.py:243
  103.8 1.1 collective-permute-start.11
  106.9 0.9 copy-done.1
  107.8 21.1 %stage0.1.refs_6_ = f32[64,128,128]{2,1,0:T(8,128)} custom-call(s32[64]{0:T(128)} %reshape_squeeze.3.table, s32[8]{0:T(128)} %bitcast.21, s32[8,192]{1,0:T(8,128)} %fusion.1.packed, bf16[64,128,128]{2,1,0:T(8,128)(2,1)} %bitcast.19, bf16[64,128,128]{2,1,0:T(8,128)(2,1)} %copy-done, bf16[64,128,128]{2,1,0:T(8,128)(2,1)} %collective-permute-done.1.refs_2_, ...), custom_call_target="tpu_custom_call" | custom-call | tf_op jit(solution)/shard_map/stage0/pallas_call | solution.py:133
  128.9 5.8 %stage1.1 = bf16[64,128,128]{2,1,0:T(8,128)(2,1)} custom-call(s32[64]{0:T(128)} %reshape_squeeze.3.table, s32[8]{0:T(128)} %bitcast.22, s32[8,192]{1,0:T(8,128)} %fusion.1.packed, bf16[64,128,128]{2,1,0:T(8,128)(2,1)} %copy-done, bf16[64,128,128]{2,1,0:T(8,128)(2,1)} %collective-permute-done.2.refs_3_.refs_1_, ...), custom_call_target="tpu_custom_call" | custom-call | tf_op jit(solution)/shard_map/stage1/pallas_call | solution.py:133
  (52 shorter events, 4.7 us)
Async XLA Ops:
  0.0 39.6 %copy-start.2 = (bf16[1,1,64,128,128]{4,3,2,1,0:T(8,128)(2,1)S(1)}, bf16[1,1,64,128,128]{4,3,2,1,0:T(8,128)(2,1)}, u32[]{:S(2)}) copy-start(bf16[1,1,64,128,128]{4,3,2,1,0:T(8,128)(2,1)} %param.7) | copy-start | bytes 6291460
  0.0 47.8 %collective-permute-start.3 = (bf16[64,128,128]{2,1,0:T(8,128)(2,1)}, bf16[64,128,128]{2,1,0:T(8,128)(2,1)}, u32[]{:S(2)}, u32[]{:S(2)}) collective-permute-start(bf16[64,128,128]{2,1,0:T(8,128)(2,1)} %bitcast.17), channel_id=1, source_target_pairs={{0,16},{1,17},{2,18},{3,19},{4,20},{5,21},{6,22},{7,23},{8,24},{9,... | collective-permute-start | bytes 6291464 | tf_op jit(solution)/shard_map/Ay/ppermute | solution.py:243
  2.1 46.9 %collective-permute-start.1 = (bf16[64,128,128]{2,1,0:T(8,128)(2,1)}, bf16[64,128,128]{2,1,0:T(8,128)(2,1)}, u32[]{:S(2)}, u32[]{:S(2)}) collective-permute-start(bf16[64,128,128]{2,1,0:T(8,128)(2,1)} %bitcast.18), channel_id=1, source_target_pairs={{0,8},{1,9},{2,10},{3,11},{4,12},{5,13},{6,14},{7,15},{8,0},{9,1},... | collective-permute-start | bytes 6291464 | tf_op jit(solution)/shard_map/Ax/ppermute | solution.py:243
  4.8 18.0 %collective-permute-start.12 = (bf16[24,128,128]{2,1,0:T(8,128)(2,1)S(1)}, bf16[24,128,128]{2,1,0:T(8,128)(2,1)S(1)}, u32[]{:S(2)}, u32[]{:S(2)}) collective-permute-start(bf16[24,128,128]{2,1,0:T(8,128)(2,1)S(1)} %get-tuple-element.5), channel_id=1, source_target_pairs={{0,1},{1,0},{2,3},{3,2},{4,5},{5,4},{6,7},{7,6},{8,9},{9,8},{10,11... | collective-permute-start | bytes 2359304 | tf_op jit(solution)/shard_map/O0/ppermute | solution.py:243
  6.2 100.0 %copy-start.11 = (s32[1,1,8,192]{3,2,1,0:T(8,128)S(1)}, s32[1,1,8,192]{3,2,1,0:T(8,128)}, u32[]{:S(2)}) copy-start(s32[1,1,8,192]{3,2,1,0:T(8,128)} %param.11) | copy-start | bytes 18436
  6.2 100.0 %copy-start.12 = (s32[1,1,8,192]{3,2,1,0:T(8,128)S(1)}, s32[1,1,8,192]{3,2,1,0:T(8,128)}, u32[]{:S(2)}) copy-start(s32[1,1,8,192]{3,2,1,0:T(8,128)} %param.9) | copy-start | bytes 18436
  6.2 100.0 %copy-start.13 = (s32[1,1,8,192]{3,2,1,0:T(8,128)S(1)}, s32[1,1,8,192]{3,2,1,0:T(8,128)}, u32[]{:S(2)}) copy-start(s32[1,1,8,192]{3,2,1,0:T(8,128)} %param.10) | copy-start | bytes 18436
  6.2 100.0 %copy-start.14 = (s32[1,1,8]{2,1,0:T(1,128)S(1)}, s32[1,1,8]{2,1,0:T(1,128)}, u32[]{:S(2)}) copy-start(s32[1,1,8]{2,1,0:T(1,128)} %param.12) | copy-start | bytes 100
  6.2 33.4 %collective-permute-start.9 = (bf16[24,128,128]{2,1,0:T(8,128)(2,1)S(1)}, bf16[24,128,128]{2,1,0:T(8,128)(2,1)S(1)}, u32[]{:S(2)}, u32[]{:S(2)}) collective-permute-start(bf16[24,128,128]{2,1,0:T(8,128)(2,1)S(1)} %get-tuple-element.6), channel_id=1, source_target_pairs={{0,1},{1,0},{2,3},{3,2},{4,5},{5,4},{6,7},{7,6},{8,9},{9,8},{10,11... | collective-permute-start | bytes 2359304 | tf_op jit(solution)/shard_map/O1/ppermute | solution.py:243
  6.4 35.3 %collective-permute-start.13 = (bf16[24,128,128]{2,1,0:T(8,128)(2,1)S(1)}, bf16[24,128,128]{2,1,0:T(8,128)(2,1)S(1)}, u32[]{:S(2)}, u32[]{:S(2)}) collective-permute-start(bf16[24,128,128]{2,1,0:T(8,128)(2,1)S(1)} %get-tuple-element.5), channel_id=1, source_target_pairs={{0,4},{1,2},{2,1},{3,7},{4,0},{5,6},{6,5},{7,3},{8,12},{9,10},{10,... | collective-permute-start | bytes 2359304 | tf_op jit(solution)/shard_map/I0/ppermute | solution.py:243
  22.8 19.0 %collective-permute-start.14 = (bf16[24,128,128]{2,1,0:T(8,128)(2,1)S(1)}, bf16[24,128,128]{2,1,0:T(8,128)(2,1)S(1)}, u32[]{:S(2)}, u32[]{:S(2)}) collective-permute-start(bf16[24,128,128]{2,1,0:T(8,128)(2,1)S(1)} %get-tuple-element.6), channel_id=1, source_target_pairs={{0,4},{1,2},{2,1},{3,7},{4,0},{5,6},{6,5},{7,3},{8,12},{9,10},{10,... | collective-permute-start | bytes 2359304 | tf_op jit(solution)/shard_map/I1/ppermute | solution.py:243
  39.7 45.0 %collective-permute-start = (bf16[64,128,128]{2,1,0:T(8,128)(2,1)S(1)}, bf16[64,128,128]{2,1,0:T(8,128)(2,1)S(1)}, u32[]{:S(2)}, u32[]{:S(2)}) collective-permute-start(bf16[64,128,128]{2,1,0:T(8,128)(2,1)S(1)} %bitcast.20), channel_id=1, source_target_pairs={{0,4},{1,5},{2,6},{3,7},{4,0},{5,1},{6,2},{7,3},{8,12},{9,13},{10,... | collective-permute-start | bytes 6291464 | tf_op jit(solution)/shard_map/W0/ppermute | solution.py:243
  41.7 10.8 %collective-permute-start.17 = (bf16[24,128,128]{2,1,0:T(8,128)(2,1)S(1)}, bf16[24,128,128]{2,1,0:T(8,128)(2,1)S(1)}, u32[]{:S(2)}, u32[]{:S(2)}) collective-permute-start(bf16[24,128,128]{2,1,0:T(8,128)(2,1)S(1)} %collective-permute-done.12.refs_11_), channel_id=1, source_target_pairs={{0,4},{1,2},{2,1},{3,7},{4,0},{5,6},{6,5},{7,3},{8,12},{9,10},{10,... | collective-permute-start | bytes 2359304 | tf_op jit(solution)/shard_map/F0/ppermute | solution.py:243
  41.8 12.0 %collective-permute-start.10 = (bf16[24,128,128]{2,1,0:T(8,128)(2,1)S(1)}, bf16[24,128,128]{2,1,0:T(8,128)(2,1)}, u32[]{:S(2)}, u32[]{:S(2)}) collective-permute-start(bf16[24,128,128]{2,1,0:T(8,128)(2,1)S(1)} %collective-permute-done.9.refs_12_), channel_id=1, source_target_pairs={{0,4},{1,2},{2,1},{3,7},{4,0},{5,6},{6,5},{7,3},{8,12},{9,10},{10,... | collective-permute-start | bytes 2359304 | tf_op jit(solution)/shard_map/F1/ppermute | solution.py:243
  47.8 17.9 %collective-permute-start.15 = (bf16[24,128,128]{2,1,0:T(8,128)(2,1)S(1)}, bf16[24,128,128]{2,1,0:T(8,128)(2,1)S(1)}, u32[]{:S(2)}, u32[]{:S(2)}) collective-permute-start(bf16[24,128,128]{2,1,0:T(8,128)(2,1)S(1)} %collective-permute-done.13.refs_13_), channel_id=1, source_target_pairs={{0,1},{1,0},{2,3},{3,2},{4,5},{5,4},{6,7},{7,6},{8,9},{9,8},{10,11... | collective-permute-start | bytes 2359304 | tf_op jit(solution)/shard_map/S0/ppermute | solution.py:243
  48.9 33.5 %collective-permute-start.16 = (bf16[24,128,128]{2,1,0:T(8,128)(2,1)S(1)}, bf16[24,128,128]{2,1,0:T(8,128)(2,1)S(1)}, u32[]{:S(2)}, u32[]{:S(2)}) collective-permute-start(bf16[24,128,128]{2,1,0:T(8,128)(2,1)S(1)} %collective-permute-done.14.refs_14_), channel_id=1, source_target_pairs={{0,1},{1,0},{2,3},{3,2},{4,5},{5,4},{6,7},{7,6},{8,9},{9,8},{10,11... | collective-permute-start | bytes 2359304 | tf_op jit(solution)/shard_map/S1/ppermute | solution.py:243
  52.6 33.2 %collective-permute-start.5 = (bf16[32,128,128]{2,1,0:T(8,128)(2,1)S(1)}, bf16[32,128,128]{2,1,0:T(8,128)(2,1)}, u32[]{:S(2)}, u32[]{:S(2)}) collective-permute-start(bf16[32,128,128]{2,1,0:T(8,128)(2,1)S(1)} %slice.20), channel_id=1, source_target_pairs={{0,8},{1,9},{2,10},{3,11},{4,12},{5,13},{6,14},{7,15},{8,0},{9,1},... | collective-permute-start | bytes 3145736 | tf_op jit(solution)/shard_map/Ad0/ppermute | solution.py:243
  53.8 32.3 %collective-permute-start.7 = (bf16[32,128,128]{2,1,0:T(8,128)(2,1)S(1)}, bf16[32,128,128]{2,1,0:T(8,128)(2,1)}, u32[]{:S(2)}, u32[]{:S(2)}) collective-permute-start(bf16[32,128,128]{2,1,0:T(8,128)(2,1)S(1)} %slice.21), channel_id=1, source_target_pairs={{0,16},{1,17},{2,18},{3,19},{4,20},{5,21},{6,22},{7,23},{8,24},{9,... | collective-permute-start | bytes 3145736 | tf_op jit(solution)/shard_map/Ad1/ppermute | solution.py:243
  65.7 41.1 %collective-permute-start.2 = (bf16[64,128,128]{2,1,0:T(8,128)(2,1)}, bf16[64,128,128]{2,1,0:T(8,128)(2,1)}, u32[]{:S(2)}, u32[]{:S(2)}) collective-permute-start(bf16[64,128,128]{2,1,0:T(8,128)(2,1)} %collective-permute-done.1.refs_2_), channel_id=1, source_target_pairs={{0,4},{1,5},{2,6},{3,7},{4,0},{5,1},{6,2},{7,3},{8,12},{9,13},{10,... | collective-permute-start | bytes 6291464 | tf_op jit(solution)/shard_map/W1/ppermute | solution.py:243
  82.5 24.4 %collective-permute-start.4 = (bf16[64,128,128]{2,1,0:T(8,128)(2,1)}, bf16[64,128,128]{2,1,0:T(8,128)(2,1)}, u32[]{:S(2)}, u32[]{:S(2)}) collective-permute-start(bf16[64,128,128]{2,1,0:T(8,128)(2,1)} %collective-permute-done.3.refs_4_), channel_id=1, source_target_pairs={{0,4},{1,5},{2,6},{3,7},{4,0},{5,1},{6,2},{7,3},{8,12},{9,13},{10,... | collective-permute-start | bytes 6291464 | tf_op jit(solution)/shard_map/W2/ppermute | solution.py:243
  84.6 19.1 %collective-permute-start.18 = (bf16[24,128,128]{2,1,0:T(8,128)(2,1)S(1)}, bf16[24,128,128]{2,1,0:T(8,128)(2,1)S(1)}, u32[]{:S(2)}, u32[]{:S(2)}) collective-permute-start(bf16[24,128,128]{2,1,0:T(8,128)(2,1)S(1)} %collective-permute-done.17.refs_17_), channel_id=1, source_target_pairs={{0,1},{1,0},{2,3},{3,2},{4,5},{5,4},{6,7},{7,6},{8,9},{9,8},{10,11... | collective-permute-start | bytes 2359304 | tf_op jit(solution)/shard_map/T0/ppermute | solution.py:243
  85.8 21.1 %collective-permute-start.6 = (bf16[32,128,128]{2,1,0:T(8,128)(2,1)}, bf16[32,128,128]{2,1,0:T(8,128)(2,1)S(1)}, u32[]{:S(2)}, u32[]{:S(2)}) collective-permute-start(bf16[32,128,128]{2,1,0:T(8,128)(2,1)} %collective-permute-done.5.refs_6_), channel_id=1, source_target_pairs={{0,4},{1,5},{2,6},{3,7},{4,0},{5,1},{6,2},{7,3},{8,12},{9,13},{10,... | collective-permute-start | bytes 3145736 | tf_op jit(solution)/shard_map/W3/ppermute | solution.py:243
  86.1 20.7 %collective-permute-start.8 = (bf16[32,128,128]{2,1,0:T(8,128)(2,1)}, bf16[32,128,128]{2,1,0:T(8,128)(2,1)}, u32[]{:S(2)}, u32[]{:S(2)}) collective-permute-start(bf16[32,128,128]{2,1,0:T(8,128)(2,1)} %collective-permute-done.7.refs_7_), channel_id=1, source_target_pairs={{0,4},{1,5},{2,6},{3,7},{4,0},{5,1},{6,2},{7,3},{8,12},{9,13},{10,... | collective-permute-start | bytes 3145736 | tf_op jit(solution)/shard_map/W3/ppermute | solution.py:243
  103.8 25.2 %collective-permute-start.11 = (bf16[24,128,128]{2,1,0:T(8,128)(2,1)}, bf16[24,128,128]{2,1,0:T(8,128)(2,1)}, u32[]{:S(2)}, u32[]{:S(2)}) collective-permute-start(bf16[24,128,128]{2,1,0:T(8,128)(2,1)} %collective-permute-done.10.refs_18_), channel_id=1, source_target_pairs={{0,1},{1,0},{2,3},{3,2},{4,5},{5,4},{6,7},{7,6},{8,9},{9,8},{10,11... | collective-permute-start | bytes 2359304 | tf_op jit(solution)/shard_map/T1/ppermute | solution.py:243
  (10 other events, 182.5 us)
